TPU v7x, 32 devices: a whole 2x2x4 slice. The times are simulated.
32 devices in a mesh: comp: 4 (over y, x), dom: 8 (over z, core).
Axes of the slice: x: 2, y: 2, z: 4, core: 2. Of those that a mesh axis runs over, the one named last changes fastest.
Arguments:
- densities: float32 [4, 3072, 2048], P('comp', 'dom'), may hold values from -6 to 6
- levels: int32 [4, 2], P('comp'), may hold values from 0 to 3
- coeffs: int32 [4], P('comp'), may hold values from -1 to 1, as said below
Outputs:
- result: float32 [4, 3072, 2048], P('comp', 'dom')
Inputs may be any that keep to these rules, and one draw needn't show every extreme that they name: `coeffs`: each coefficient is -1 or 1; both values occur.
All inputs are finite; a program needn't handle non-finite values.
Results may differ from a plain program's by a relative error of at most 0.0001.
Values sent between devices are 32-bit elements; how exact they have to be, the bound alone decides.
No kernel may reach another device: no remote copies, remote signals or barrier semaphores. Data moves between devices by JAX's collectives and lax.ppermute only.
A program may use at most 64 MiB of HBM per device.

v0:
```python
import functools

import jax
import jax.numpy as jnp
import ml_dtypes
import numpy as np
from jax import lax
from jax.experimental import pallas as pl
from jax.experimental.pallas import tpu as pltpu
from jax.sharding import PartitionSpec as P

MX = 2048
MV = 256
PRE = 8
POST = 2
LANES = 128
HALO = 16
AXES = ("comp", "dom")
F32 = jnp.float32
BF16 = jnp.bfloat16


def split_table(table):
    high = table.astype(ml_dtypes.bfloat16)
    low = (table - high.astype(np.float64)).astype(ml_dtypes.bfloat16)
    return high, low


def cosine_table(length, mode_ids, positions):
    scale = np.where(mode_ids == 0, np.sqrt(1.0 / length), np.sqrt(2.0 / length))
    turns = ((2 * positions[:, None] + 1) * mode_ids[None, :]) % (4 * length)
    return np.cos(np.pi * turns / (2.0 * length)) * scale[None, :]


def split(value):
    high = value.astype(BF16)
    return high, (value - high.astype(F32)).astype(BF16)


def dot(a, b, dims=((1,), (0,))):
    return lax.dot_general(a, b, (dims, ((), ())), preferred_element_type=F32)


def rates(levels_ref):
    level_x, level_v = levels_ref[0, 0], levels_ref[0, 1]
    courant = 0.3 + level_x.astype(F32) / 15.0
    diffusion = 0.1 + level_v.astype(F32) / 30.0
    return level_x, courant, diffusion


def fill_coefs(coef, blocks, courant, diffusion, scale, last):
    cells = blocks * LANES
    lane = lax.broadcasted_iota(jnp.int32, (8, LANES), 1)
    for c in range(blocks):
        at = (lane + c * LANES).astype(F32)
        speed = courant * jnp.abs(-1.0 + (2.0 * at + 1.0) / cells)
        own = 1.0 - speed - 2.0 * diffusion
        factor = scale if last else 1.0 / diffusion
        coef[0, c] = own * factor
        coef[1, c] = speed * factor


def step(buf, side, edge, coef, base, stride, unrolls, spread=None):
    blocks = buf.shape[0]
    half = blocks // 2
    lane = lax.broadcasted_iota(jnp.int32, (8, LANES), 1)
    first, final = lane == 0, lane == LANES - 1

    def load(c, r):
        return buf[c, pl.ds(base + r, 8, stride=stride), :]

    def store(c, r, value):
        buf[c, pl.ds(base + r, 8, stride=stride), :] = value

    def right(v):
        return pltpu.roll(v, 1, axis=1)

    def left(v):
        return pltpu.roll(v, LANES - 1, axis=1)

    def combine(r, low, cur, windward, left_edge, right_edge):
        count = len(cur)
        rights = [right(v) for v in cur]
        lefts = [left(v) for v in cur]
        for b in range(count):
            from_left = jnp.where(first, left_edge if b == 0 else rights[b - 1], rights[b])
            from_right = jnp.where(final, right_edge if b == count - 1 else lefts[b + 1], lefts[b])
            around = from_left + from_right
            if spread is not None:
                around = around * spread
            c = low + b
            store(c, r, coef[0, c] * cur[b] + coef[1, c] * windward[b] + around)

    for c in range(half):
        edge[c] = load(c, stride)

    def negative(r, cur, windward):
        side[r] = cur[half - 1]
        combine(r, 0, cur, windward, cur[0], left(load(half, r)))

    def negative_rows(i, cur):
        for u in range(unrolls[0]):
            r = i * unrolls[0] + u
            following = [load(c, r + 1) for c in range(half)]
            negative(r, cur, following)
            cur = following
        return cur

    assert (stride - 1) % unrolls[0] == 0 and stride % unrolls[1] == 0
    cur = lax.fori_loop(0, (stride - 1) // unrolls[0], negative_rows, [load(c, 0) for c in range(half)])
    negative(stride - 1, cur, [edge[c] for c in range(half)])

    def positive_rows(i, before):
        for u in range(unrolls[1]):
            r = i * unrolls[1] + u
            cur = [load(half + b, r) for b in range(half)]
            combine(r, half, cur, before, right(side[r]), cur[half - 1])
            before = cur
        return before

    lax.fori_loop(0, stride // unrolls[1], positive_rows, [load(half + b, -1) for b in range(half)])


def advance_kernel(
    levels, cells, above, below, bv_high, bv_low, advanced, reduced, buf, side, edge, coef, high, low, sems, *, stride
):
    blocks = buf.shape[0]
    rows = cells.shape[0]
    copies = []
    for c in range(blocks):
        lanes = pl.ds(c * LANES, LANES)
        for source, at, size in ((cells, HALO, rows), (above, 0, HALO), (below, HALO + rows, HALO)):
            copies.append(pltpu.make_async_copy(source.at[:, lanes], buf.at[c, pl.ds(at, size), :], sems.at[0]))
    for copy in copies:
        copy.start()
    level_x, courant, diffusion = rates(levels)
    count = jnp.clip(PRE - 3 + level_x, 0, PRE)
    scale = lax.fori_loop(0, count - 1, lambda i, s: s * diffusion, jnp.float32(1.0))
    fill_coefs(coef, blocks, courant, diffusion, None, False)
    for copy in copies:
        copy.wait()
    base = HALO + rows // 2 - 4 * stride
    unrolls = (5, 3)

    def inner(i, carry):
        step(buf, side, edge, coef, base, stride, unrolls)
        return carry

    lax.fori_loop(0, count - 1, inner, 0)
    fill_coefs(coef, blocks, courant, diffusion, scale, True)
    step(buf, side, edge, coef, base, stride, unrolls, scale * diffusion)
    out = pltpu.make_async_copy(buf, advanced, sems.at[1])
    out.start()
    for c in range(blocks):
        lanes = pl.ds(c * LANES, LANES)
        high[:, lanes], low[:, lanes] = split(buf[c, pl.ds(HALO, rows), :])
    total = dot(high[...], bv_high[...]) + dot(high[...], bv_low[...]) + dot(low[...], bv_high[...])
    reduced[...] = total.T
    out.wait()


def reverse_lanes(value):
    lane = lax.broadcasted_iota(jnp.int32, value.shape, 1)
    return jnp.take_along_axis(value, LANES - 1 - lane, axis=1)


def combine_kernel(
    meta, reduced, even_high, even_low, odd_high, odd_low, corrected, halo,
    eh_buf, el_buf, oh_buf, ol_buf, even, odd, sems, *, groups, slabs, modes,
):
    tables = ((even_high, eh_buf), (even_low, el_buf), (odd_high, oh_buf), (odd_low, ol_buf))
    copies = [pltpu.make_async_copy(s, d, sems.at[i]) for i, (s, d) in enumerate(tables)]
    for copy in copies:
        copy.start()
    slab_rows = reduced.shape[2]
    parts = slab_rows // LANES
    for g in range(groups):
        rows = pl.ds(8 * g, 8)
        for d in range(slabs // 2):
            for j in range(parts):
                ahead = reduced[g * slabs + d, :, pl.ds(j * LANES, LANES)]
                mirrored = reverse_lanes(
                    reduced[g * slabs + slabs - 1 - d, :, pl.ds((parts - 1 - j) * LANES, LANES)]
                )
                lanes = pl.ds(d * slab_rows + j * LANES, LANES)
                even[rows, lanes] = ahead + mirrored
                odd[rows, lanes] = ahead - mirrored
    own = lax.axis_index(AXES[0]) * slabs + lax.axis_index(AXES[1])
    half_modes = eh_buf.shape[1]
    size = 8 * groups
    row_mode = own * modes + lax.broadcasted_iota(jnp.int32, (8, half_modes), 0)
    column = lax.broadcasted_iota(jnp.int32, (8, half_modes), 1)
    halves = []
    for parity, (source, high_buf, low_buf) in enumerate(((even, eh_buf, el_buf), (odd, oh_buf, ol_buf))):
        high, low = split(source[...])
        copies[2 * parity].wait()
        both = dot(jnp.concatenate([high, low], axis=0), high_buf[...])
        copies[2 * parity + 1].wait()
        projected = both[:size] + both[size:] + dot(high, low_buf[...])
        mode_x = (2 * column + parity).astype(F32)
        surpluses = []
        combined = jnp.zeros((8, half_modes), F32)
        for g in range(groups):
            factor_x = (1 << (3 - meta[g, 0])).astype(F32)
            factor_v = (1 << (3 - meta[g, 1])).astype(F32)
            damping_x = 1.0 / (1.0 + (mode_x * factor_x / MX) ** 2)
            damping_v = 1.0 / (1.0 + (row_mode.astype(F32) * factor_v / MV) ** 2)
            surplus = damping_x * projected[8 * g : 8 * g + 8] * damping_v
            surpluses.append(surplus)
            combined = combined + meta[g, 2].astype(F32) * surplus
        high, low = split(jnp.concatenate([combined - s for s in surpluses], axis=0))
        both = dot(jnp.concatenate([high, low], axis=0), high_buf[...], ((1,), (1,)))
        halves.append(both[:size] + both[size:] + dot(high, low_buf[...], ((1,), (1,))))
    even[...] = halves[0]
    odd[...] = halves[1]
    for g in range(groups):
        rows = pl.ds(8 * g, 8)
        for d in range(slabs // 2):
            for j in range(parts):
                lanes = pl.ds(d * slab_rows + j * LANES, LANES)
                e, o = even[rows, lanes], odd[rows, lanes]
                corrected[g * slabs + d, :, pl.ds(j * LANES, LANES)] = e + o
                corrected[g * slabs + slabs - 1 - d, :, pl.ds((parts - 1 - j) * LANES, LANES)] = reverse_lanes(e - o)
    lane = lax.broadcasted_iota(jnp.int32, (8, LANES), 1)
    for g in range(groups):
        for d in range(slabs):
            before = corrected[g * slabs + (d - 1) % slabs, :, pl.ds((parts - 1) * LANES, LANES)]
            after = corrected[g * slabs + (d + 1) % slabs, :, pl.ds(0, LANES)]
            halo[g * slabs + d] = jnp.where(
                lane < POST, pltpu.roll(before, POST, axis=1), pltpu.roll(after, POST, axis=1)
            )


def correct_kernel(
    levels, advanced, corrected, halo, bvt_high, bvt_low, result, buf, side, edge, coef, sems, *, stride
):
    blocks = buf.shape[0]
    rows = result.shape[0]
    fetch = pltpu.make_async_copy(advanced, buf, sems.at[0])
    fetch.start()
    _, courant, diffusion = rates(levels)
    fill_coefs(coef, blocks, courant, diffusion, None, False)
    wide = jnp.concatenate([corrected[...], halo[...]], axis=1)
    high, low = split(wide.T[: rows + 8])
    fetch.wait()
    width = 2 * LANES
    for c in range(0, blocks, 2):
        lanes = pl.ds(c * LANES, width)
        right_high, right_low = bvt_high[:, lanes], bvt_low[:, lanes]
        change = dot(high, right_high) + dot(high, right_low) + dot(low, right_high)
        for k in range(2):
            part = change[:, k * LANES : (k + 1) * LANES]
            buf[c + k, pl.ds(HALO, rows), :] += part[:rows]
            buf[c + k, pl.ds(HALO - POST, POST), :] += part[rows : rows + POST]
            buf[c + k, pl.ds(HALO + rows, POST), :] += part[rows + POST : rows + 2 * POST]
    base = HALO + rows // 2 - 4 * stride
    unrolls = (6, 7)
    for _ in range(POST - 1):
        step(buf, side, edge, coef, base, stride, unrolls)
    scale = jnp.float32(1.0)
    for _ in range(POST - 1):
        scale = scale * diffusion
    fill_coefs(coef, blocks, courant, diffusion, scale, True)
    step(buf, side, edge, coef, base, stride, unrolls, scale * diffusion)
    copies = [
        pltpu.make_async_copy(
            buf.at[c, pl.ds(HALO, rows), :], result.at[:, pl.ds(c * LANES, LANES)], sems.at[1]
        )
        for c in range(blocks)
    ]
    for copy in copies:
        copy.start()
    for copy in copies:
        copy.wait()


def body(densities, levels, coeffs):
    density = densities[0]
    rows, cells = density.shape
    groups, slabs = lax.axis_size("comp"), lax.axis_size("dom")
    devices = groups * slabs
    modes = MV // devices
    blocks = cells // LANES
    assert modes * devices == MV and modes <= 8 and slabs % 2 == 0 and blocks % 4 == 0
    half_x, half_modes = rows * slabs // 2, MX // 2

    table = cosine_table(cells, np.arange(MV), np.arange(cells))
    bv_high, bv_low = split_table(table)
    bvt_high, bvt_low = split_table(np.ascontiguousarray(table.T))
    tables_x = []
    for parity in range(2):
        tables_x += split_table(cosine_table(2 * half_x, 2 * np.arange(half_modes) + parity, np.arange(half_x)))

    vmem = pl.BlockSpec(memory_space=pltpu.VMEM)
    smem = pl.BlockSpec(memory_space=pltpu.SMEM)
    hbm = pl.BlockSpec(memory_space=pl.ANY)
    ring = [(i, (i + 1) % slabs) for i in range(slabs)]
    above = lax.ppermute(density[rows - HALO :], "dom", ring)
    below = lax.ppermute(density[:HALO], "dom", [(b, a) for a, b in ring])

    tall = rows + 2 * HALO

    def scratch(stride):
        return [
            pltpu.VMEM((blocks, tall, LANES), F32),
            pltpu.VMEM((stride, 8, LANES), F32),
            pltpu.VMEM((blocks // 2, 8, LANES), F32),
            pltpu.VMEM((2, blocks, 8, LANES), F32),
        ]

    stride = (rows + 2 * (PRE + POST)) // 8 + 1
    advanced, reduced = pl.pallas_call(
        functools.partial(advance_kernel, stride=stride),
        out_shape=(
            jax.ShapeDtypeStruct((blocks, tall, LANES), F32),
            jax.ShapeDtypeStruct((MV, rows), F32),
        ),
        in_specs=[smem, hbm, hbm, hbm, vmem, vmem],
        out_specs=(hbm, vmem),
        scratch_shapes=scratch(stride)
        + [pltpu.VMEM((rows, cells), BF16), pltpu.VMEM((rows, cells), BF16), pltpu.SemaphoreType.DMA((2,))],
        name="advance",
    )(levels, density, above, below, bv_high, bv_low)

    parcels = jnp.pad(reduced.reshape(devices, modes, rows), ((0, 0), (0, 8 - modes), (0, 0)))
    parcels = lax.all_to_all(parcels, AXES, 0, 0, tiled=True)
    note = jnp.concatenate([levels[0], coeffs])
    note = jnp.broadcast_to(jnp.pad(note, (0, LANES - 3)), (groups, 1, LANES))
    meta = lax.all_to_all(note, "comp", 0, 0, tiled=True).reshape(groups, LANES)

    corrected, halo = pl.pallas_call(
        functools.partial(combine_kernel, groups=groups, slabs=slabs, modes=modes),
        out_shape=(
            jax.ShapeDtypeStruct((devices, 8, rows), F32),
            jax.ShapeDtypeStruct((devices, 8, LANES), F32),
        ),
        in_specs=[smem, vmem, hbm, hbm, hbm, hbm],
        out_specs=(vmem, vmem),
        scratch_shapes=[pltpu.VMEM((half_x, half_modes), BF16)] * 4
        + [pltpu.VMEM((8 * groups, half_x), F32)] * 2
        + [pltpu.SemaphoreType.DMA((4,))],
        name="combine",
    )(meta, parcels, *tables_x)

    corrected = lax.all_to_all(corrected, AXES, 0, 0, tiled=True)
    corrected = corrected[:, :modes].reshape(MV, rows)
    ends = halo[:, :modes, : 2 * POST].reshape(devices, 1, modes * 2 * POST)
    ends = lax.all_to_all(ends, AXES, 0, 0, tiled=True).reshape(MV, 2 * POST)
    ends = jnp.pad(ends, ((0, 0), (0, LANES - 2 * POST)))

    stride = (rows + 2 * POST) // 8 + 1
    result = pl.pallas_call(
        functools.partial(correct_kernel, stride=stride),
        out_shape=jax.ShapeDtypeStruct((rows, cells), F32),
        in_specs=[smem, hbm, vmem, vmem, vmem, vmem],
        out_specs=hbm,
        scratch_shapes=scratch(stride) + [pltpu.SemaphoreType.DMA((2,))],
        name="correct",
    )(levels, advanced, corrected, ends, bvt_high, bvt_low)
    return result[None]


def solution(mesh):
    placed = (P("comp", "dom", None), P("comp", None), P("comp"))
    return jax.shard_map(
        body, mesh=mesh, in_specs=placed, out_specs=P("comp", "dom", None), check_vma=False
    )
```

profile of v0, /device:TPU:0, one launch (start us, length us, event | category | flops | bytes accessed | tf_op | source)
XLA Modules:
  0.0 117.3 jit_solution(2724825881648165857)
XLA Ops:
  0.0 1.0 slice_bitcast_fusion
  1.0 4.6 %collective-permute-start.1 = (f32[16,2048]{1,0:T(8,128)S(1)}, f32[16,2048]{1,0:T(8,128)S(1)}, u32[]{:S(2)}, u32[]{:S(2)}) collective-permute-start(f32[16,2048]{1,0:T(8,128)S(1)} %get-tuple-element.13), channel_id=1, source_target_pairs={{1,0},{2,1},{3,2},{4,3},{5,4},{6,5},{7,6},{0,7},{9,8},{10,9},{11,1... | collective-permute-start | bytes 393224 | tf_op jit(solution)/shard_map/ppermute | solution.py:299
  5.6 0.0 collective-permute-start
  6.2 0.7 pad_add_fusion
  7.0 0.6 broadcast_in_dim.6
  7.5 3.7 %all-to-all-start = ((s32[4,1,128]{2,1,0:T(1,128)}), s32[4,1,128]{2,1,0:T(1,128)S(1)}, u32[]{:S(2)}, u32[]{:S(2)}) async-start(s32[4,1,128]{2,1,0:T(1,128)} %broadcast_in_dim.6), calls=%async_computation | async-start | bytes 4096 | tf_op jit(solution)/shard_map/all_to_all | solution.py:329
  11.3 0.0 collective-permute-done.1.below
  11.3 0.0 copy-start.1
  11.3 0.5 collective-permute-done.above
  11.8 0.0 copy-start.2
  11.8 0.2 copy-done.1
  11.9 0.5 copy-done.2
  12.4 25.3 %advance.1 = (f32[16,416,128]{2,1,0:T(8,128)}, f32[256,384]{1,0:T(8,128)}) custom-call(s32[1,2]{1,0:T(1,128)} %levels.3, f32[384,2048]{1,0:T(8,128)} %bitcast.12, f32[16,2048]{1,0:T(8,128)} %copy-done.2, f32[16,2048]{1,0:T(8,128)} %copy-done.1, bf16[2048,256]{1,0:T(8,128)(2,1)} %constant.20.clone.bv_high, bf16[2048,256]{1,0:T(8,128)(2,1)} %constant.21.clone.bv_low), custom_call_target="tpu_custom_call" | custom-call | tf_op jit(solution)/shard_map/advance/pallas_call | solution.py:312
  37.7 0.0 all-to-all-done
  37.7 0.0 copy-start.3
  37.8 29.4 %all_to_all.20.reduced = f32[32,8,384]{2,1,0:T(8,128)} all-to-all(f32[32,8,384]{2,1,0:T(8,128)} %bitcast.14), channel_id=1, replica_groups=mesh['comp'=4,'dom'=8] {'comp','dom'}, dimensions={0} | all-to-all | bytes 786432 | tf_op jit(solution)/shard_map/all_to_all | solution.py:326
  67.2 0.0 copy-done.3
  67.2 10.4 %combine.1 = (f32[32,8,384]{2,1,0:T(8,128)}, f32[32,8,128]{2,1,0:T(8,128)}) custom-call(s32[4,128]{1,0:T(4,128)} %bitcast.17, f32[32,8,384]{2,1,0:T(8,128)} %all_to_all.20.reduced, bf16[1536,1024]{1,0:T(8,128)(2,1)} %constant.22.clone.even_high, bf16[1536,1024]{1,0:T(8,128)(2,1)} %constant.23.clone.even_low, bf16[1536,1024]{1,0:T(8,128)(2,1)} %constant.24.clone.odd_high, ...), custom_call_target="tpu_custom_call" | custom-call | tf_op jit(solution)/shard_map/combine/pallas_call | solution.py:331
  77.5 1.0 copy.14
  78.6 0.1 copy.15
  78.6 9.3 %all_to_all.21 = f32[32,1,32]{2,1,0:T(1,128)S(1)} all-to-all(f32[32,1,32]{2,1,0:T(1,128)S(1)} %copy.15), channel_id=1, replica_groups=mesh['comp'=4,'dom'=8] {'comp','dom'}, dimensions={0} | all-to-all | bytes 8192 | tf_op jit(solution)/shard_map/all_to_all | solution.py:348
  87.9 2.6 %all-to-all-start.2 = ((f32[32,8,384]{2,1,0:T(8,128)}), f32[32,8,384]{2,1,0:T(8,128)S(1)}, u32[]{:S(2)}, u32[]{:S(2)}) async-start(f32[32,8,384]{2,1,0:T(8,128)} %get-tuple-element.11), calls=%async_computation.2 | async-start | bytes 786432 | tf_op jit(solution)/shard_map/all_to_all | solution.py:345
  90.5 0.5 broadcast.7
  91.0 0.7 reduce.3
  91.7 0.1 reshape.21
  91.8 0.7 pad.9.halo
  92.5 11.4 %all-to-all-done.2 = f32[32,8,384]{2,1,0:T(8,128)S(1)} async-done(((f32[32,8,384]{2,1,0:T(8,128)}), f32[32,8,384]{2,1,0:T(8,128)S(1)}, u32[]{:S(2)}, u32[]{:S(2)}) %all-to-all-start.2) | async-done | bytes 393248 | tf_op jit(solution)/shard_map/all_to_all | solution.py:345
  103.9 0.0 copy-start
  103.9 0.7 copy-done
  104.7 12.6 %correct.1 = f32[384,2048]{1,0:T(8,128)} custom-call(s32[1,2]{1,0:T(1,128)} %levels.3, f32[16,416,128]{2,1,0:T(8,128)} %get-tuple-element.9.advanced, f32[256,384]{1,0:T(8,128)} %bitcast.13, f32[256,128]{1,0:T(8,128)} %pad.9.halo, bf16[256,2048]{1,0:T(8,128)(2,1)} %constant.26.clone.bvt_high, bf16[256,2048]{1,0:T(8,128)(2,1)} %constant.27.clone.bvt_low), custom_call_target="tpu_custom_call" | custom-call | tf_op jit(solution)/shard_map/correct/pallas_call | solution.py:352
  (1 shorter events, 0.0 us)
Async XLA Ops:
  1.0 10.3 %collective-permute-start.1 = (f32[16,2048]{1,0:T(8,128)S(1)}, f32[16,2048]{1,0:T(8,128)S(1)}, u32[]{:S(2)}, u32[]{:S(2)}) collective-permute-start(f32[16,2048]{1,0:T(8,128)S(1)} %get-tuple-element.13), channel_id=1, source_target_pairs={{1,0},{2,1},{3,2},{4,3},{5,4},{6,5},{7,6},{0,7},{9,8},{10,9},{11,1... | collective-permute-start | bytes 393224 | tf_op jit(solution)/shard_map/ppermute | solution.py:299
  5.6 6.2 %collective-permute-start = (f32[16,2048]{1,0:T(8,128)S(1)}, f32[16,2048]{1,0:T(8,128)S(1)}, u32[]{:S(2)}, u32[]{:S(2)}) collective-permute-start(f32[16,2048]{1,0:T(8,128)S(1)} %get-tuple-element.14), channel_id=1, source_target_pairs={{0,1},{1,2},{2,3},{3,4},{4,5},{5,6},{6,7},{7,0},{8,9},{9,10},{10,1... | collective-permute-start | bytes 393224 | tf_op jit(solution)/shard_map/ppermute | solution.py:298
  7.5 30.2 %all-to-all-start = ((s32[4,1,128]{2,1,0:T(1,128)}), s32[4,1,128]{2,1,0:T(1,128)S(1)}, u32[]{:S(2)}, u32[]{:S(2)}) async-start(s32[4,1,128]{2,1,0:T(1,128)} %broadcast_in_dim.6), calls=%async_computation | async-start | bytes 4096 | tf_op jit(solution)/shard_map/all_to_all | solution.py:329
  11.3 0.7 copy-start.1
  11.8 0.7 copy-start.2
  37.7 29.4 %copy-start.3 = (s32[4,1,128]{2,1,0:T(1,128)}, s32[4,1,128]{2,1,0:T(1,128)S(1)}, u32[]{:S(2)}) copy-start(s32[4,1,128]{2,1,0:T(1,128)S(1)} %all-to-all-done) | copy-start | bytes 6148
  87.9 16.0 %all-to-all-start.2 = ((f32[32,8,384]{2,1,0:T(8,128)}), f32[32,8,384]{2,1,0:T(8,128)S(1)}, u32[]{:S(2)}, u32[]{:S(2)}) async-start(f32[32,8,384]{2,1,0:T(8,128)} %get-tuple-element.11), calls=%async_computation.2 | async-start | bytes 786432 | tf_op jit(solution)/shard_map/all_to_all | solution.py:345
  103.9 0.7 copy-start
where the time goes:
time: 117 us
  Pallas kernels  48.3 us (41%)
  blocking collectives  38.7 us (33%)
  waiting for transfers between devices  11.9 us (10%)
  starting transfers between devices  10.9 us (9%)
  local copies, waits for them, and re-layouts  5.37 us (5%)
  other arithmetic  1.4 us (1%)
    all_to_all x1, blocking collectives, body(): parcels = lax.all_to_all(parcels, AXES, 0, 0, tiled=True)  29.4 us
    pallas_call x1, Pallas kernels, body(): pl.pallas_call(functools.partial(advance_kernel, stride=stride), out_shap...  25.3 us
    pallas_call x1, Pallas kernels, body(): pl.pallas_call(functools.partial(correct_kernel, stride=stride), out_shap...  12.6 us
    all_to_all x1, waiting for transfers between devices, body(): corrected = lax.all_to_all(corrected, AXES, 0, 0, tiled=True)  11.4 us
    pallas_call x1, Pallas kernels, body(): pl.pallas_call(functools.partial(combine_kernel, groups=groups, slabs=sla...  10.4 us
    all_to_all x1, blocking collectives, body(): ends = lax.all_to_all(ends, AXES, 0, 0, tiled=True).reshape(MV, 2 * POST)  9.28 us
    ppermute x1, starting transfers between devices, body(): below = lax.ppermute(density[:HALO], 'dom', [(b, a) for a, b in ring])  4.57 us
    all_to_all x1, starting transfers between devices, body(): meta = lax.all_to_all(note, 'comp', 0, 0, tiled=True).reshape(groups, LANES)  3.72 us
  transfers between devices with their start and end apart: 4, of which 2 were waited for; matrix products, arithmetic and copies ran while one was open for 3% of the time, Pallas kernels for 22%

commit v1 on v0

v1 whole, which is shorter than its diff:
```python
import functools

import jax
import jax.numpy as jnp
import ml_dtypes
import numpy as np
from jax import lax
from jax.experimental import pallas as pl
from jax.experimental.pallas import tpu as pltpu
from jax.sharding import PartitionSpec as P

MX = 2048
MV = 256
PRE = 8
POST = 2
LANES = 128
HALO = 16
PHASES = 4
MARGIN = 8
GUARD = 8
AXES = ("comp", "dom")
F32 = jnp.float32
BF16 = jnp.bfloat16


def split_table(table):
    high = table.astype(ml_dtypes.bfloat16)
    low = (table - high.astype(np.float64)).astype(ml_dtypes.bfloat16)
    return high, low


def cosine_table(length, mode_ids, positions):
    scale = np.where(mode_ids == 0, np.sqrt(1.0 / length), np.sqrt(2.0 / length))
    turns = ((2 * positions[:, None] + 1) * mode_ids[None, :]) % (4 * length)
    return np.cos(np.pi * turns / (2.0 * length)) * scale[None, :]


def split(value):
    high = value.astype(BF16)
    return high, (value - high.astype(F32)).astype(BF16)


def dot(a, b, dims=((1,), (0,))):
    return lax.dot_general(a, b, (dims, ((), ())), preferred_element_type=F32)


def rates(levels_ref):
    level_x, level_v = levels_ref[0, 0], levels_ref[0, 1]
    courant = 0.3 + level_x.astype(F32) / 15.0
    diffusion = 0.1 + level_v.astype(F32) / 30.0
    return level_x, courant, diffusion


def fill_coefs(coef, cells, courant, diffusion):
    size = 128
    inverse = 1.0 / diffusion

    def rows(i, carry):
        at = (i * size + lax.broadcasted_iota(jnp.int32, (size, LANES), 0)).astype(F32)
        speed = courant * jnp.abs(-1.0 + (2.0 * at + 1.0) / cells)
        where = pl.ds(pl.multiple_of(GUARD + i * size, 8), size)
        coef[0, where, :] = (1.0 - speed - 2.0 * diffusion) * inverse
        coef[1, where, :] = speed * inverse
        return carry

    lax.fori_loop(0, cells // size, rows, 0)


def mirror_edges(buf, cells):
    for t in range(PHASES):
        buf[t, pl.ds(GUARD - 1, 1), :] = buf[t, pl.ds(GUARD, 1), :]
        buf[t, pl.ds(GUARD + cells, 1), :] = buf[t, pl.ds(GUARD + cells - 1, 1), :]


def stepped(src, coef, row, size, leftward):
    here = pl.ds(row, size)
    own, windward = coef[0, here, :], coef[1, here, :]
    cur = [src[t, here, :] for t in range(PHASES)]
    if leftward:
        wind = cur[1:] + [pltpu.roll(cur[0], LANES - 1, axis=1)]
    else:
        wind = [pltpu.roll(cur[-1], 1, axis=1)] + cur[:-1]
    return [
        own * cur[t]
        + windward * wind[t]
        + (src[t, pl.ds(row - 1, size), :] + src[t, pl.ds(row + 1, size), :])
        for t in range(PHASES)
    ]


def inner_step(src, dst, coef, cells):
    unroll = 32
    for leftward in (True, False):
        start = GUARD if leftward else GUARD + cells // 2

        def rows(i, carry):
            for k in range(unroll):
                row = pl.multiple_of(start + (i * unroll + k) * 8, 8)
                for t, value in enumerate(stepped(src, coef, row, 8, leftward)):
                    dst[t, pl.ds(row, 8), :] = value
            return carry

        lax.fori_loop(0, cells // 16 // unroll, rows, 0)
    mirror_edges(dst, cells)


def moved_lanes(pieces):
    out = None
    for source, origin, target, count in pieces:
        shift = (target - origin) % LANES
        moved = pltpu.roll(source, shift, axis=1) if shift else source
        if out is None:
            out = moved
        else:
            lane = lax.broadcasted_iota(jnp.int32, moved.shape, 1)
            out = jnp.where((lane >= target) & (lane < target + count), moved, out)
    return out


def overlaps(rows):
    quarter = rows // PHASES
    runs = []
    for j in range(rows // LANES):
        for t in range(PHASES):
            low, high = max(LANES * j, quarter * t), min(LANES * (j + 1), quarter * (t + 1))
            if low < high:
                runs.append((j, t, low - LANES * j, MARGIN + low - quarter * t, high - low))
    return runs


def packed_lane(rows, x):
    return (x % PHASES) * (rows // PHASES) + x // PHASES


def advance_kernel(
    levels, cells, above, below, bvt_high, bvt_low, advanced, reduced,
    natural, first, second, third, coef, high, low, fetches, sems,
):
    rows, width = cells.shape
    planes = width // LANES
    start = PHASES * MARGIN
    fetched = []
    for c in range(planes):
        lanes = pl.ds(c * LANES, LANES)
        copies = [
            pltpu.make_async_copy(source.at[:, lanes], natural.at[c, pl.ds(at, size), :], fetches.at[c])
            for source, at, size in ((cells, start, rows), (above, start - HALO, HALO), (below, start + rows, HALO))
        ]
        for copy in copies:
            copy.start()
        fetched.append(copies)
    level_x, courant, diffusion = rates(levels)
    count = jnp.clip(PRE - 3 + level_x, 0, PRE)
    scale = lax.fori_loop(0, count, lambda i, s: s * diffusion, jnp.float32(1.0))
    fill_coefs(coef, width, courant, diffusion)
    top, tail = start - HALO, start + rows + HALO
    for c in range(planes):
        natural[c, pl.ds(0, top), :] = jnp.zeros((top, LANES), F32)
        natural[c, pl.ds(tail, PHASES * LANES - tail), :] = jnp.zeros((PHASES * LANES - tail, LANES), F32)
        for copy in fetched[c]:
            copy.wait()
        for t in range(PHASES):
            first[t, pl.ds(GUARD + c * LANES, LANES), :] = natural[c, pl.ds(t, LANES, stride=PHASES), :].T
    mirror_edges(first, width)
    inner = count - 1

    def pair(i, carry):
        inner_step(first, second, coef, width)
        inner_step(second, first, coef, width)
        return carry

    lax.fori_loop(0, inner // 2, pair, 0)

    def final(src):
        unroll = 16
        for leftward in (True, False):
            begin = 0 if leftward else width // 2

            def body(i, carry):
                for k in range(unroll):
                    row = pl.multiple_of(begin + (i * unroll + k) * 16, 16)
                    for t, value in enumerate(stepped(src, coef, GUARD + row, 16, leftward)):
                        value = value * scale
                        third[t, pl.ds(row, 16), :] = value
                        lanes = pl.ds(t * LANES, LANES)
                        high[pl.ds(row, 16), lanes], low[pl.ds(row, 16), lanes] = split(value)
                return carry

            lax.fori_loop(0, width // 32 // unroll, body, 0)

    @pl.when(inner % 2 == 1)
    def _():
        inner_step(first, second, coef, width)
        final(second)

    @pl.when(inner % 2 == 0)
    def _():
        final(first)

    out = pltpu.make_async_copy(third, advanced, sems.at[0])
    out.start()
    total = dot(bvt_high[...], high[...]) + dot(bvt_low[...], high[...]) + dot(bvt_high[...], low[...])
    for j in range(rows // LANES):
        pieces = [
            (total[:, t * LANES : (t + 1) * LANES], own, packed, n) for b, t, packed, own, n in overlaps(rows) if b == j
        ]
        reduced[:, pl.ds(j * LANES, LANES)] = moved_lanes(pieces)
    out.wait()


def reverse_lanes(value):
    lane = lax.broadcasted_iota(jnp.int32, value.shape, 1)
    return jnp.take_along_axis(value, LANES - 1 - lane, axis=1)


def combine_kernel(
    meta, reduced, even_high, even_low, odd_high, odd_low, corrected, halo,
    eh_buf, el_buf, oh_buf, ol_buf, even, odd, sems, *, groups, slabs, modes,
):
    tables = ((even_high, eh_buf), (even_low, el_buf), (odd_high, oh_buf), (odd_low, ol_buf))
    copies = [pltpu.make_async_copy(s, d, sems.at[i]) for i, (s, d) in enumerate(tables)]
    for copy in copies:
        copy.start()
    slab_rows = reduced.shape[2]
    parts = slab_rows // LANES
    for g in range(groups):
        rows = pl.ds(8 * g, 8)
        for d in range(slabs // 2):
            for j in range(parts):
                ahead = reduced[g * slabs + d, :, pl.ds(j * LANES, LANES)]
                mirrored = reverse_lanes(
                    reduced[g * slabs + slabs - 1 - d, :, pl.ds((parts - 1 - j) * LANES, LANES)]
                )
                lanes = pl.ds(d * slab_rows + j * LANES, LANES)
                even[rows, lanes] = ahead + mirrored
                odd[rows, lanes] = ahead - mirrored
    own = lax.axis_index(AXES[0]) * slabs + lax.axis_index(AXES[1])
    half_modes = eh_buf.shape[1]
    size = 8 * groups
    row_mode = own * modes + lax.broadcasted_iota(jnp.int32, (8, half_modes), 0)
    column = lax.broadcasted_iota(jnp.int32, (8, half_modes), 1)
    halves = []
    for parity, (source, high_buf, low_buf) in enumerate(((even, eh_buf, el_buf), (odd, oh_buf, ol_buf))):
        high, low = split(source[...])
        copies[2 * parity].wait()
        both = dot(jnp.concatenate([high, low], axis=0), high_buf[...])
        copies[2 * parity + 1].wait()
        projected = both[:size] + both[size:] + dot(high, low_buf[...])
        mode_x = (2 * column + parity).astype(F32)
        surpluses = []
        combined = jnp.zeros((8, half_modes), F32)
        for g in range(groups):
            factor_x = (1 << (3 - meta[g, 0])).astype(F32)
            factor_v = (1 << (3 - meta[g, 1])).astype(F32)
            damping_x = 1.0 / (1.0 + (mode_x * factor_x / MX) ** 2)
            damping_v = 1.0 / (1.0 + (row_mode.astype(F32) * factor_v / MV) ** 2)
            surplus = damping_x * projected[8 * g : 8 * g + 8] * damping_v
            surpluses.append(surplus)
            combined = combined + meta[g, 2].astype(F32) * surplus
        high, low = split(jnp.concatenate([combined - s for s in surpluses], axis=0))
        both = dot(jnp.concatenate([high, low], axis=0), high_buf[...], ((1,), (1,)))
        halves.append(both[:size] + both[size:] + dot(high, low_buf[...], ((1,), (1,))))
    even[...] = halves[0]
    odd[...] = halves[1]
    for g in range(groups):
        rows = pl.ds(8 * g, 8)
        for d in range(slabs // 2):
            for j in range(parts):
                lanes = pl.ds(d * slab_rows + j * LANES, LANES)
                e, o = even[rows, lanes], odd[rows, lanes]
                corrected[g * slabs + d, :, pl.ds(j * LANES, LANES)] = e + o
                corrected[g * slabs + slabs - 1 - d, :, pl.ds((parts - 1 - j) * LANES, LANES)] = reverse_lanes(e - o)
    for g in range(groups):
        for d in range(slabs):
            pieces = []
            for h, x in enumerate(halo_rows(slab_rows)):
                other = (d - 1) % slabs if x < 0 else (d + 1) % slabs
                at = packed_lane(slab_rows, x % slab_rows)
                block = corrected[g * slabs + other, :, pl.ds(at // LANES * LANES, LANES)]
                pieces.append((block, at % LANES, h, 1))
            halo[g * slabs + d] = moved_lanes(pieces)


def halo_rows(rows):
    return [x for x in range(-POST, 0)] + [rows + x for x in range(POST)]


def correct_kernel(
    levels, advanced, corrected, halo, bv_high, bv_low, result, first, second, coef, work, natural, fetches, sems
):
    rows, width = result.shape
    planes = width // LANES
    fetched = [
        pltpu.make_async_copy(advanced.at[t], first.at[t, pl.ds(GUARD, width), :], fetches.at[t]) for t in range(PHASES)
    ]
    for copy in fetched:
        copy.start()
    _, courant, diffusion = rates(levels)
    fill_coefs(coef, width, courant, diffusion)
    scale = jnp.float32(1.0)
    for _ in range(POST):
        scale = scale * diffusion
    wide = []
    for t in range(PHASES):
        pieces = [
            (corrected[:, pl.ds(j * LANES, LANES)], packed, own, n) for j, b, packed, own, n in overlaps(rows) if b == t
        ]
        for h, x in enumerate(halo_rows(rows)):
            if (x + PHASES * MARGIN) % PHASES == t:
                pieces.append((halo[...], h, (x + PHASES * MARGIN) // PHASES, 1))
        wide.append(moved_lanes(pieces))
    high, low = split(jnp.concatenate(wide, axis=1))
    for copy in fetched:
        copy.wait()
    size = 2 * LANES
    for i in range(width // size):
        where = pl.ds(i * size, size)
        left_high, left_low = bv_high[where, :], bv_low[where, :]
        change = dot(left_high, high) + dot(left_high, low) + dot(left_low, high)
        for t in range(PHASES):
            first[t, pl.ds(GUARD + i * size, size), :] += change[:, t * LANES : (t + 1) * LANES]
    mirror_edges(first, width)
    source, other = first, second
    for _ in range(POST - 1):
        inner_step(source, other, coef, width)
        source, other = other, source
    copies = []
    for c in range(planes):
        for k in range(LANES // 8):
            for t, value in enumerate(stepped(source, coef, GUARD + c * LANES + 8 * k, 8, c < planes // 2)):
                work[c % 2, t, pl.ds(8 * k, 8), :] = value * scale
        for t in range(PHASES):
            back = work[c % 2, t].T
            natural[c, pl.ds(t, rows // PHASES, stride=PHASES), :] = back[MARGIN : MARGIN + rows // PHASES]
        copies.append(pltpu.make_async_copy(natural.at[c], result.at[:, pl.ds(c * LANES, LANES)], sems.at[0]))
        copies[-1].start()
    for copy in copies:
        copy.wait()


def body(densities, levels, coeffs):
    density = densities[0]
    rows, cells = density.shape
    groups, slabs = lax.axis_size("comp"), lax.axis_size("dom")
    devices = groups * slabs
    modes = MV // devices
    blocks = cells // LANES
    assert modes * devices == MV and modes <= 8 and slabs % 2 == 0 and blocks % 4 == 0
    half_x, half_modes = rows * slabs // 2, MX // 2

    table = cosine_table(cells, np.arange(MV), np.arange(cells))
    bv_high, bv_low = split_table(table)
    bvt_high, bvt_low = split_table(np.ascontiguousarray(table.T))
    packed = np.arange(rows)
    packed = PHASES * (packed % (rows // PHASES)) + packed // (rows // PHASES)
    positions = (rows * np.arange(slabs // 2)[:, None] + packed[None, :]).reshape(-1)
    tables_x = []
    for parity in range(2):
        tables_x += split_table(cosine_table(2 * half_x, 2 * np.arange(half_modes) + parity, positions))

    vmem = pl.BlockSpec(memory_space=pltpu.VMEM)
    smem = pl.BlockSpec(memory_space=pltpu.SMEM)
    hbm = pl.BlockSpec(memory_space=pl.ANY)
    ring = [(i, (i + 1) % slabs) for i in range(slabs)]
    above = lax.ppermute(density[rows - HALO :], "dom", ring)
    below = lax.ppermute(density[:HALO], "dom", [(b, a) for a, b in ring])

    assert rows % LANES == 0 and rows + HALO <= PHASES * (LANES - MARGIN) and PRE + POST <= HALO
    tall = pltpu.VMEM((PHASES, cells + 2 * GUARD, LANES), F32)
    coefs = pltpu.VMEM((2, cells + 2 * GUARD, LANES), F32)
    flat = pltpu.VMEM((cells, PHASES * LANES), BF16)
    advanced, reduced = pl.pallas_call(
        advance_kernel,
        out_shape=(
            jax.ShapeDtypeStruct((PHASES, cells, LANES), F32),
            jax.ShapeDtypeStruct((MV, rows), F32),
        ),
        in_specs=[smem, hbm, hbm, hbm, vmem, vmem],
        out_specs=(hbm, vmem),
        scratch_shapes=[
            pltpu.VMEM((blocks, PHASES * LANES, LANES), F32),
            tall,
            tall,
            pltpu.VMEM((PHASES, cells, LANES), F32),
            coefs,
            flat,
            flat,
            pltpu.SemaphoreType.DMA((blocks,)),
            pltpu.SemaphoreType.DMA((1,)),
        ],
        name="advance",
    )(levels, density, above, below, bvt_high, bvt_low)

    parcels = jnp.pad(reduced.reshape(devices, modes, rows), ((0, 0), (0, 8 - modes), (0, 0)))
    parcels = lax.all_to_all(parcels, AXES, 0, 0, tiled=True)
    note = jnp.concatenate([levels[0], coeffs])
    note = jnp.broadcast_to(jnp.pad(note, (0, LANES - 3)), (groups, 1, LANES))
    meta = lax.all_to_all(note, "comp", 0, 0, tiled=True).reshape(groups, LANES)

    corrected, halo = pl.pallas_call(
        functools.partial(combine_kernel, groups=groups, slabs=slabs, modes=modes),
        out_shape=(
            jax.ShapeDtypeStruct((devices, 8, rows), F32),
            jax.ShapeDtypeStruct((devices, 8, LANES), F32),
        ),
        in_specs=[smem, vmem, hbm, hbm, hbm, hbm],
        out_specs=(vmem, vmem),
        scratch_shapes=[pltpu.VMEM((half_x, half_modes), BF16)] * 4
        + [pltpu.VMEM((8 * groups, half_x), F32)] * 2
        + [pltpu.SemaphoreType.DMA((4,))],
        name="combine",
    )(meta, parcels, *tables_x)

    corrected = lax.all_to_all(corrected, AXES, 0, 0, tiled=True)
    corrected = corrected[:, :modes].reshape(MV, rows)
    ends = halo[:, :modes, : 2 * POST].reshape(devices, 1, modes * 2 * POST)
    ends = lax.all_to_all(ends, AXES, 0, 0, tiled=True).reshape(MV, 2 * POST)
    ends = jnp.pad(ends, ((0, 0), (0, LANES - 2 * POST)))

    result = pl.pallas_call(
        correct_kernel,
        out_shape=jax.ShapeDtypeStruct((rows, cells), F32),
        in_specs=[smem, hbm, vmem, vmem, vmem, vmem],
        out_specs=hbm,
        scratch_shapes=[
            tall,
            tall,
            coefs,
            pltpu.VMEM((2, PHASES, LANES, LANES), F32),
            pltpu.VMEM((blocks, rows, LANES), F32),
            pltpu.SemaphoreType.DMA((PHASES,)),
            pltpu.SemaphoreType.DMA((1,)),
        ],
        name="correct",
    )(levels, advanced, corrected, ends, bv_high, bv_low)
    return result[None]


def solution(mesh):
    placed = (P("comp", "dom", None), P("comp", None), P("comp"))
    return jax.shard_map(
        body, mesh=mesh, in_specs=placed, out_specs=P("comp", "dom", None), check_vma=False
    )
```

time: 117 us -> 93.7 us (0.80)
  Pallas kernels: 48.3 us -> 33.8 us
  blocking collectives: 38.7 us -> 29 us
    pallas_call x2, Pallas kernels: 38 us -> 23.4 us  [the longest x1 14.6 us: body(): pl.pallas_call(advance_kernel, out_shape=(jax.ShapeDtypeStruct((PHASES, c...]
    all_to_all x1, blocking collectives: 29.4 us -> 19.7 us  [body(): parcels = lax.all_to_all(parcels, AXES, 0, 0, tiled=True)]
  transfers between devices with their start and end apart: 4 -> 4, of which waited for: 2 -> 2; matrix products, arithmetic and copies ran while one was open for 3% -> 4% of each run, Pallas kernels for 22% -> 16%
where the time goes in v1:
time: 93.7 us; the launch traced here: 93.2 us
  Pallas kernels  33.8 us (36%)
  blocking collectives  29 us (31%)
  waiting for transfers between devices  11.7 us (12%)
  starting transfers between devices  11.1 us (12%)
  local copies, waits for them, and re-layouts  5.38 us (6%)
  other arithmetic  1.45 us (2%)
    all_to_all x1, blocking collectives, body(): parcels = lax.all_to_all(parcels, AXES, 0, 0, tiled=True)  19.7 us
    pallas_call x1, Pallas kernels, body(): pl.pallas_call(advance_kernel, out_shape=(jax.ShapeDtypeStruct((PHASES, c...  14.6 us
    all_to_all x1, waiting for transfers between devices, body(): corrected = lax.all_to_all(corrected, AXES, 0, 0, tiled=True)  11.2 us
    pallas_call x1, Pallas kernels, body(): pl.pallas_call(functools.partial(combine_kernel, groups=groups, slabs=sla...  10.4 us
    all_to_all x1, blocking collectives, body(): ends = lax.all_to_all(ends, AXES, 0, 0, tiled=True).reshape(MV, 2 * POST)  9.28 us
    pallas_call x1, Pallas kernels, body(): pl.pallas_call(correct_kernel, out_shape=jax.ShapeDtypeStruct((rows, cell...  8.79 us
    ppermute x1, starting transfers between devices, body(): below = lax.ppermute(density[:HALO], 'dom', [(b, a) for a, b in ring])  4.57 us
    all_to_all x1, starting transfers between devices, body(): meta = lax.all_to_all(note, 'comp', 0, 0, tiled=True).reshape(groups, LANES)  3.72 us
  transfers between devices with their start and end apart: 4, of which 2 were waited for; matrix products, arithmetic and copies ran while one was open for 4% of the time, Pallas kernels for 16%

profile of v1, /device:TPU:0, one launch (start us, length us, event | category | flops | bytes accessed | tf_op | source)
XLA Modules:
  0.0 93.2 jit_solution(3899974075477464053)
XLA Ops:
  0.0 1.0 %slice_bitcast_fusion = (f32[16,2048]{1,0:T(8,128)S(1)}, f32[16,2048]{1,0:T(8,128)S(1)}) fusion(f32[1,384,2048]{2,1,0:T(8,128)} %param.11), kind=kLoop, calls=%fused_computation | loop fusion | bytes 524288 | tf_op jit(solution)/shard_map/slice | solution.py:366
  1.0 4.6 %collective-permute-start.1 = (f32[16,2048]{1,0:T(8,128)S(1)}, f32[16,2048]{1,0:T(8,128)S(1)}, u32[]{:S(2)}, u32[]{:S(2)}) collective-permute-start(f32[16,2048]{1,0:T(8,128)S(1)} %get-tuple-element.13), channel_id=1, source_target_pairs={{1,0},{2,1},{3,2},{4,3},{5,4},{6,5},{7,6},{0,7},{9,8},{10,9},{11,1... | collective-permute-start | bytes 393224 | tf_op jit(solution)/shard_map/ppermute | solution.py:366
  5.6 0.0 collective-permute-start
  6.2 0.7 pad_add_fusion
  7.0 0.6 broadcast_in_dim.6
  7.5 3.7 %all-to-all-start = ((s32[4,1,128]{2,1,0:T(1,128)}), s32[4,1,128]{2,1,0:T(1,128)S(1)}, u32[]{:S(2)}, u32[]{:S(2)}) async-start(s32[4,1,128]{2,1,0:T(1,128)} %broadcast_in_dim.6), calls=%async_computation | async-start | bytes 4096 | tf_op jit(solution)/shard_map/all_to_all | solution.py:398
  11.2 0.0 collective-permute-done.1.below
  11.2 0.0 copy-start.1
  11.2 0.5 collective-permute-done.above
  11.8 0.0 copy-start.2
  11.8 0.1 copy-done.1
  11.9 0.5 copy-done.2
  12.4 14.6 %advance.1 = (f32[4,2048,128]{2,1,0:T(8,128)}, f32[256,384]{1,0:T(8,128)}) custom-call(s32[1,2]{1,0:T(1,128)} %levels.3, f32[384,2048]{1,0:T(8,128)} %bitcast.12, f32[16,2048]{1,0:T(8,128)} %copy-done.2, f32[16,2048]{1,0:T(8,128)} %copy-done.1, bf16[256,2048]{1,0:T(8,128)(2,1)} %constant.20.clone.bvt_high, bf16[256,2048]{1,0:T(8,128)(2,1)} %constant.21.clone.bvt_low), custom_call_target="tpu_custom_call" | custom-call | tf_op jit(solution)/shard_map/advance/pallas_call | solution.py:372
  27.0 0.0 all-to-all-done
  27.0 0.0 copy-start.3
  27.1 19.7 %all_to_all.20.reduced = f32[32,8,384]{2,1,0:T(8,128)} all-to-all(f32[32,8,384]{2,1,0:T(8,128)} %bitcast.14), channel_id=1, replica_groups=mesh['comp'=4,'dom'=8] {'comp','dom'}, dimensions={0} | all-to-all | bytes 786432 | tf_op jit(solution)/shard_map/all_to_all | solution.py:395
  46.7 0.0 copy-done.3
  46.8 10.4 %combine.1 = (f32[32,8,384]{2,1,0:T(8,128)}, f32[32,8,128]{2,1,0:T(8,128)}) custom-call(s32[4,128]{1,0:T(4,128)} %bitcast.17, f32[32,8,384]{2,1,0:T(8,128)} %all_to_all.20.reduced, bf16[1536,1024]{1,0:T(8,128)(2,1)} %constant.22.clone.even_high, bf16[1536,1024]{1,0:T(8,128)(2,1)} %constant.23.clone.even_low, bf16[1536,1024]{1,0:T(8,128)(2,1)} %constant.24.clone.odd_high, ...), custom_call_target="tpu_custom_call" | custom-call | tf_op jit(solution)/shard_map/combine/pallas_call | solution.py:400
  57.1 1.0 %copy.14 = f32[32,8,4]{0,2,1:T(4,128)S(1)} copy(f32[32,8,4]{2,1,0:T(8,128)} %bitcast.15) | data formatting | bytes 8192 | tf_op jit(solution)/shard_map/slice | solution.py:416
  58.1 0.1 copy.15
  58.2 9.3 %all_to_all.21 = f32[32,1,32]{2,1,0:T(1,128)S(1)} all-to-all(f32[32,1,32]{2,1,0:T(1,128)S(1)} %copy.15), channel_id=1, replica_groups=mesh['comp'=4,'dom'=8] {'comp','dom'}, dimensions={0} | all-to-all | bytes 8192 | tf_op jit(solution)/shard_map/all_to_all | solution.py:417
  67.5 2.8 %all-to-all-start.2 = ((f32[32,8,384]{2,1,0:T(8,128)}), f32[32,8,384]{2,1,0:T(8,128)S(1)}, u32[]{:S(2)}, u32[]{:S(2)}) async-start(f32[32,8,384]{2,1,0:T(8,128)} %get-tuple-element.11), calls=%async_computation.2 | async-start | bytes 786432 | tf_op jit(solution)/shard_map/all_to_all | solution.py:414
  70.3 0.6 broadcast.7
  70.9 0.7 reduce.3
  71.6 0.1 reshape.21
  71.7 0.7 pad.9.halo
  72.4 11.2 %all-to-all-done.2 = f32[32,8,384]{2,1,0:T(8,128)S(1)} async-done(((f32[32,8,384]{2,1,0:T(8,128)}), f32[32,8,384]{2,1,0:T(8,128)S(1)}, u32[]{:S(2)}, u32[]{:S(2)}) %all-to-all-start.2) | async-done | bytes 393248 | tf_op jit(solution)/shard_map/all_to_all | solution.py:414
  83.5 0.0 copy-start
  83.5 0.7 copy-done
  84.3 8.8 %correct.1 = f32[384,2048]{1,0:T(8,128)} custom-call(s32[1,2]{1,0:T(1,128)} %levels.3, f32[4,2048,128]{2,1,0:T(8,128)} %get-tuple-element.9.advanced, f32[256,384]{1,0:T(8,128)} %bitcast.13, f32[256,128]{1,0:T(8,128)} %pad.9.halo, bf16[2048,256]{1,0:T(8,128)(2,1)} %constant.26.clone.bv_high, bf16[2048,256]{1,0:T(8,128)(2,1)} %constant.27.clone.bv_low), custom_call_target="tpu_custom_call" | custom-call | tf_op jit(solution)/shard_map/correct/pallas_call | solution.py:420
  (1 shorter events, 0.0 us)
Async XLA Ops:
  1.0 10.2 %collective-permute-start.1 = (f32[16,2048]{1,0:T(8,128)S(1)}, f32[16,2048]{1,0:T(8,128)S(1)}, u32[]{:S(2)}, u32[]{:S(2)}) collective-permute-start(f32[16,2048]{1,0:T(8,128)S(1)} %get-tuple-element.13), channel_id=1, source_target_pairs={{1,0},{2,1},{3,2},{4,3},{5,4},{6,5},{7,6},{0,7},{9,8},{10,9},{11,1... | collective-permute-start | bytes 393224 | tf_op jit(solution)/shard_map/ppermute | solution.py:366
  5.6 6.2 %collective-permute-start = (f32[16,2048]{1,0:T(8,128)S(1)}, f32[16,2048]{1,0:T(8,128)S(1)}, u32[]{:S(2)}, u32[]{:S(2)}) collective-permute-start(f32[16,2048]{1,0:T(8,128)S(1)} %get-tuple-element.14), channel_id=1, source_target_pairs={{0,1},{1,2},{2,3},{3,4},{4,5},{5,6},{6,7},{7,0},{8,9},{9,10},{10,1... | collective-permute-start | bytes 393224 | tf_op jit(solution)/shard_map/ppermute | solution.py:365
  7.5 19.5 %all-to-all-start = ((s32[4,1,128]{2,1,0:T(1,128)}), s32[4,1,128]{2,1,0:T(1,128)S(1)}, u32[]{:S(2)}, u32[]{:S(2)}) async-start(s32[4,1,128]{2,1,0:T(1,128)} %broadcast_in_dim.6), calls=%async_computation | async-start | bytes 4096 | tf_op jit(solution)/shard_map/all_to_all | solution.py:398
  11.2 0.7 copy-start.1
  11.8 0.6 copy-start.2
  27.0 19.7 %copy-start.3 = (s32[4,1,128]{2,1,0:T(1,128)}, s32[4,1,128]{2,1,0:T(1,128)S(1)}, u32[]{:S(2)}) copy-start(s32[4,1,128]{2,1,0:T(1,128)S(1)} %all-to-all-done) | copy-start | bytes 6148
  67.5 16.0 %all-to-all-start.2 = ((f32[32,8,384]{2,1,0:T(8,128)}), f32[32,8,384]{2,1,0:T(8,128)S(1)}, u32[]{:S(2)}, u32[]{:S(2)}) async-start(f32[32,8,384]{2,1,0:T(8,128)} %get-tuple-element.11), calls=%async_computation.2 | async-start | bytes 786432 | tf_op jit(solution)/shard_map/all_to_all | solution.py:414
  83.5 0.7 copy-start

commit v2 on v1

--- a/solution.py
+++ b/solution.py
@@ -128,13 +128,17 @@
     return runs
 
 
+def parcel_rows(rows):
+    return 8 * rows // LANES + 1
+
+
 def packed_lane(rows, x):
     return (x % PHASES) * (rows // PHASES) + x // PHASES
 
 
 def advance_kernel(
-    levels, cells, above, below, bvt_high, bvt_low, advanced, reduced,
-    natural, first, second, third, coef, high, low, fetches, sems,
+    levels, coeffs, cells, above, below, bvt_high, bvt_low, advanced, parcels,
+    natural, first, second, third, coef, high, low, fetches, sems, *, devices,
 ):
     rows, width = cells.shape
     planes = width // LANES
@@ -142,13 +146,10 @@
     fetched = []
     for c in range(planes):
         lanes = pl.ds(c * LANES, LANES)
-        copies = [
-            pltpu.make_async_copy(source.at[:, lanes], natural.at[c, pl.ds(at, size), :], fetches.at[c])
-            for source, at, size in ((cells, start, rows), (above, start - HALO, HALO), (below, start + rows, HALO))
-        ]
-        for copy in copies:
-            copy.start()
-        fetched.append(copies)
+        fetched.append(
+            pltpu.make_async_copy(cells.at[:, lanes], natural.at[c, pl.ds(start, rows), :], fetches.at[c])
+        )
+        fetched[c].start()
     level_x, courant, diffusion = rates(levels)
     count = jnp.clip(PRE - 3 + level_x, 0, PRE)
     scale = lax.fori_loop(0, count, lambda i, s: s * diffusion, jnp.float32(1.0))
@@ -157,8 +158,10 @@
     for c in range(planes):
         natural[c, pl.ds(0, top), :] = jnp.zeros((top, LANES), F32)
         natural[c, pl.ds(tail, PHASES * LANES - tail), :] = jnp.zeros((PHASES * LANES - tail, LANES), F32)
-        for copy in fetched[c]:
-            copy.wait()
+        lanes = pl.ds(c * LANES, LANES)
+        natural[c, pl.ds(top, HALO), :] = above[:, lanes]
+        natural[c, pl.ds(start + rows, HALO), :] = below[:, lanes]
+        fetched[c].wait()
         for t in range(PHASES):
             first[t, pl.ds(GUARD + c * LANES, LANES), :] = natural[c, pl.ds(t, LANES, stride=PHASES), :].T
     mirror_edges(first, width)
@@ -200,85 +203,178 @@
     out = pltpu.make_async_copy(third, advanced, sems.at[0])
     out.start()
     total = dot(bvt_high[...], high[...]) + dot(bvt_low[...], high[...]) + dot(bvt_high[...], low[...])
+    modes = bvt_high.shape[0] // devices
+    lane = lax.broadcasted_iota(jnp.int32, (1, LANES), 1)
+    note = jnp.where(lane == 0, (1 << (3 - level_x)).astype(F32) / MX, 0.0)
+    note = jnp.where(lane == 1, (1 << (3 - levels[0, 1])).astype(F32) / MV, note)
+    note = jnp.where(lane == 2, coeffs[0].astype(F32), note)
+    if modes < 8:
+        parcels[...] = jnp.zeros_like(parcels)
     for j in range(rows // LANES):
         pieces = [
             (total[:, t * LANES : (t + 1) * LANES], own, packed, n) for b, t, packed, own, n in overlaps(rows) if b == j
         ]
-        reduced[:, pl.ds(j * LANES, LANES)] = moved_lanes(pieces)
+        packed = moved_lanes(pieces)
+        for q in range(devices):
+            parcels[pl.ds(parcel_rows(rows) * q + 8 * j, modes), :] = packed[modes * q : modes * (q + 1)]
+    for q in range(devices):
+        parcels[pl.ds(parcel_rows(rows) * (q + 1) - 1, 1), :] = note
     out.wait()
 
 
-def reverse_lanes(value):
-    lane = lax.broadcasted_iota(jnp.int32, value.shape, 1)
-    return jnp.take_along_axis(value, LANES - 1 - lane, axis=1)
+def rotate_sums(terms):
+    total = None
+    for factor, value in terms:
+        if abs(factor) < 1e-12:
+            continue
+        if abs(factor - 1.0) < 1e-12:
+            total = value if total is None else total + value
+        elif abs(factor + 1.0) < 1e-12:
+            total = -value if total is None else total - value
+        else:
+            part = value * np.float32(factor)
+            total = part if total is None else total + part
+    return total
+
+
+def slab_angle(slabs, d, s):
+    return np.cos(np.pi * d * s / slabs), np.sin(np.pi * d * s / slabs)
+
+
+def slabs_to_residues(cells):
+    slabs = len(cells)
+    half = slabs // 2
+    plus = {d: cells[d] + cells[slabs - d] for d in range(1, half)}
+    minus = {d: cells[d] - cells[slabs - d] for d in range(1, half)}
+    out = []
+    for s in range(slabs + 1):
+        same, other = (plus, minus) if s % 2 == 0 else (minus, plus)
+        fixed = [(1.0, cells[0])], []
+        middle = slab_angle(slabs, half, s)
+        real = fixed[0] + [(middle[0], cells[half])] + [(slab_angle(slabs, d, s)[0], same[d]) for d in range(1, half)]
+        imag = [(middle[1], cells[half])] + [(slab_angle(slabs, d, s)[1], other[d]) for d in range(1, half)]
+        out.append((rotate_sums(real), rotate_sums(imag)))
+    return out
+
+
+def residues_to_slabs(values):
+    slabs = len(values) - 1
+    out = [None] * slabs
+    for d in range(slabs // 2 + 1):
+        first, second = [], []
+        for s, (real, imag) in enumerate(values):
+            cosine, sine = slab_angle(slabs, d, s)
+            (first if s % 2 == 0 else second).append((cosine, real))
+            if imag is not None:
+                (second if s % 2 == 0 else first).append((-sine, imag))
+        one, two = rotate_sums(first), rotate_sums(second)
+        out[d] = one if two is None else one + two
+        if 0 < d < slabs // 2:
+            out[slabs - d] = one if two is None else one - two
+    return out
+
+
+def residue_table(rows, slabs, positions):
+    used = MX // (2 * slabs)
+    count = -(-used // LANES) * LANES
+    q = np.arange(count)
+    scale = np.where(q < used, np.sqrt(2.0 / (rows * slabs)), 0.0)[None, :]
+    blocks = []
+    for shift, sign in ((0, -1.0), (1, 1.0)):
+        turns = ((2 * positions[:, None] + 1) * (q + shift)[None, :]) % (2 * rows)
+        angle = np.pi * turns / rows
+        blocks.append(np.concatenate([np.cos(angle) * scale, sign * np.sin(angle) * scale], axis=0))
+    return np.concatenate(blocks, axis=1)
+
+
+def twiddle_table(rows, slabs, positions):
+    s = np.arange(slabs + 1)[:, None]
+    angle = np.pi * ((2 * positions[None, :] + 1) * s) / (2.0 * rows * slabs)
+    return np.stack([np.cos(angle), np.sin(angle)]).astype(np.float32)[:, :, None, :]
 
 
 def combine_kernel(
-    meta, reduced, even_high, even_low, odd_high, odd_low, corrected, halo,
-    eh_buf, el_buf, oh_buf, ol_buf, even, odd, sems, *, groups, slabs, modes,
+    parcels, twiddle, ahead_high, ahead_low, back_high, back_low, corrected, waves, *, groups, slabs, modes
 ):
-    tables = ((even_high, eh_buf), (even_low, el_buf), (odd_high, oh_buf), (odd_low, ol_buf))
-    copies = [pltpu.make_async_copy(s, d, sems.at[i]) for i, (s, d) in enumerate(tables)]
-    for copy in copies:
-        copy.start()
-    slab_rows = reduced.shape[2]
+    slab_rows = twiddle.shape[3]
     parts = slab_rows // LANES
+    each = parcel_rows(slab_rows)
+    block = 8 * groups
     for g in range(groups):
-        rows = pl.ds(8 * g, 8)
-        for d in range(slabs // 2):
-            for j in range(parts):
-                ahead = reduced[g * slabs + d, :, pl.ds(j * LANES, LANES)]
-                mirrored = reverse_lanes(
-                    reduced[g * slabs + slabs - 1 - d, :, pl.ds((parts - 1 - j) * LANES, LANES)]
-                )
-                lanes = pl.ds(d * slab_rows + j * LANES, LANES)
-                even[rows, lanes] = ahead + mirrored
-                odd[rows, lanes] = ahead - mirrored
+        for j in range(parts):
+            lanes = pl.ds(j * LANES, LANES)
+            cells = [parcels[pl.ds(each * (g * slabs + d) + 8 * j, 8), :] for d in range(slabs)]
+            for s, (real, imag) in enumerate(slabs_to_residues(cells)):
+                where = pl.ds(s * block + 8 * g, 8)
+                cosine, sine = twiddle[0, s, :, lanes], twiddle[1, s, :, lanes]
+                if s == 0:
+                    turned = real, jnp.zeros_like(real)
+                elif imag is None:
+                    turned = real * cosine, real * sine
+                else:
+                    turned = real * cosine - imag * sine, real * sine + imag * cosine
+                waves[where, lanes] = turned[0]
+                waves[where, pl.ds(slab_rows + j * LANES, LANES)] = turned[1]
+    high, low = split(waves[...])
+    projected = dot(high, ahead_high[...]) + dot(low, ahead_high[...]) + dot(high, ahead_low[...])
+    width = projected.shape[1]
     own = lax.axis_index(AXES[0]) * slabs + lax.axis_index(AXES[1])
-    half_modes = eh_buf.shape[1]
-    size = 8 * groups
-    row_mode = own * modes + lax.broadcasted_iota(jnp.int32, (8, half_modes), 0)
-    column = lax.broadcasted_iota(jnp.int32, (8, half_modes), 1)
-    halves = []
-    for parity, (source, high_buf, low_buf) in enumerate(((even, eh_buf, el_buf), (odd, oh_buf, ol_buf))):
-        high, low = split(source[...])
-        copies[2 * parity].wait()
-        both = dot(jnp.concatenate([high, low], axis=0), high_buf[...])
-        copies[2 * parity + 1].wait()
-        projected = both[:size] + both[size:] + dot(high, low_buf[...])
-        mode_x = (2 * column + parity).astype(F32)
+    row_mode = (own * modes + lax.broadcasted_iota(jnp.int32, (8, width), 0)).astype(F32)
+    column = lax.broadcasted_iota(jnp.int32, (8, width), 1)
+    rightward = column >= width // 2
+    notes = [parcels[pl.ds(each * (g * slabs + 1) - 1, 1), :] for g in range(groups)]
+    factors_x = [jnp.broadcast_to(note[:, 0:1], (8, width)) for note in notes]
+    dampings_v = [1.0 / (1.0 + (row_mode * note[:, 1:2]) ** 2) for note in notes]
+    weights = [jnp.broadcast_to(note[:, 2:3], (8, width)) for note in notes]
+    changes = []
+    for s in range(slabs + 1):
+        mode_x = jnp.where(
+            rightward, 2 * slabs * (column - width // 2) + 2 * slabs - s, 2 * slabs * column + s
+        )
+        keep = jnp.where(mode_x == 0, 0.5, 1.0)
+        if s in (0, slabs):
+            keep = jnp.where(rightward, 0.0, keep)
+        mode_x = mode_x.astype(F32)
         surpluses = []
-        combined = jnp.zeros((8, half_modes), F32)
+        combined = None
         for g in range(groups):
-            factor_x = (1 << (3 - meta[g, 0])).astype(F32)
-            factor_v = (1 << (3 - meta[g, 1])).astype(F32)
-            damping_x = 1.0 / (1.0 + (mode_x * factor_x / MX) ** 2)
-            damping_v = 1.0 / (1.0 + (row_mode.astype(F32) * factor_v / MV) ** 2)
-            surplus = damping_x * projected[8 * g : 8 * g + 8] * damping_v
+            damping_x = 1.0 / (1.0 + (mode_x * factors_x[g]) ** 2)
+            where = s * block + 8 * g
+            surplus = damping_x * projected[where : where + 8] * dampings_v[g] * keep
             surpluses.append(surplus)
-            combined = combined + meta[g, 2].astype(F32) * surplus
-        high, low = split(jnp.concatenate([combined - s for s in surpluses], axis=0))
-        both = dot(jnp.concatenate([high, low], axis=0), high_buf[...], ((1,), (1,)))
-        halves.append(both[:size] + both[size:] + dot(high, low_buf[...], ((1,), (1,))))
-    even[...] = halves[0]
-    odd[...] = halves[1]
+            part = weights[g] * surplus
+            combined = part if combined is None else combined + part
+        changes += [combined - surplus for surplus in surpluses]
+    high, low = split(jnp.concatenate(changes, axis=0))
+    waves[...] = dot(high, back_high[...]) + dot(low, back_high[...]) + dot(high, back_low[...])
     for g in range(groups):
-        rows = pl.ds(8 * g, 8)
-        for d in range(slabs // 2):
-            for j in range(parts):
-                lanes = pl.ds(d * slab_rows + j * LANES, LANES)
-                e, o = even[rows, lanes], odd[rows, lanes]
-                corrected[g * slabs + d, :, pl.ds(j * LANES, LANES)] = e + o
-                corrected[g * slabs + slabs - 1 - d, :, pl.ds((parts - 1 - j) * LANES, LANES)] = reverse_lanes(e - o)
+        for j in range(parts):
+            lanes = pl.ds(j * LANES, LANES)
+            values = []
+            for s in range(slabs + 1):
+                where = pl.ds(s * block + 8 * g, 8)
+                real, imag = waves[where, lanes], waves[where, pl.ds(slab_rows + j * LANES, LANES)]
+                cosine, sine = twiddle[0, s, :, lanes], twiddle[1, s, :, lanes]
+                if s == 0:
+                    values.append((real, None))
+                elif s == slabs:
+                    values.append((real * cosine + imag * sine, None))
+                else:
+                    values.append((real * cosine + imag * sine, real * sine - imag * cosine))
+            for d, value in enumerate(residues_to_slabs(values)):
+                corrected[pl.ds(each * (g * slabs + d) + 8 * j, 8), :] = value
+    lane = lax.broadcasted_iota(jnp.int32, (8, LANES), 1)
     for g in range(groups):
         for d in range(slabs):
             pieces = []
             for h, x in enumerate(halo_rows(slab_rows)):
                 other = (d - 1) % slabs if x < 0 else (d + 1) % slabs
                 at = packed_lane(slab_rows, x % slab_rows)
-                block = corrected[g * slabs + other, :, pl.ds(at // LANES * LANES, LANES)]
-                pieces.append((block, at % LANES, h, 1))
-            halo[g * slabs + d] = moved_lanes(pieces)
+                source = corrected[pl.ds(each * (g * slabs + other) + at // LANES * 8, 8), :]
+                pieces.append((source, at % LANES, h, 1))
+            ends = jnp.where(lane < 2 * POST, moved_lanes(pieces), 0.0)
+            ends = pltpu.roll(ends, 0, axis=1, stride=2 * POST, stride_axis=0)
+            corrected[pl.ds(each * (g * slabs + d + 1) - 1, 1), :] = jnp.sum(ends, axis=0, keepdims=True)
 
 
 def halo_rows(rows):
@@ -286,7 +382,8 @@
 
 
 def correct_kernel(
-    levels, advanced, corrected, halo, bv_high, bv_low, result, first, second, coef, work, natural, fetches, sems
+    levels, advanced, parcels, bv_high, bv_low, result, first, second, coef, work, natural, corrected, halo,
+    fetches, sems, *, devices,
 ):
     rows, width = result.shape
     planes = width // LANES
@@ -300,6 +397,15 @@
     scale = jnp.float32(1.0)
     for _ in range(POST):
         scale = scale * diffusion
+    each, modes = parcel_rows(rows), bv_high.shape[1] // devices
+    for q in range(devices):
+        where = pl.ds(modes * q, modes)
+        for j in range(rows // LANES):
+            corrected[where, pl.ds(j * LANES, LANES)] = parcels[pl.ds(each * q + 8 * j, modes), :]
+    ends = parcels[pl.ds(each - 1, devices, stride=each), :]
+    for m in range(modes):
+        shift = (LANES - 2 * POST * m) % LANES
+        halo[pl.ds(m, devices, stride=modes), :] = pltpu.roll(ends, shift, axis=1) if shift else ends
     wide = []
     for t in range(PHASES):
         pieces = [
@@ -345,18 +451,15 @@
     devices = groups * slabs
     modes = MV // devices
     blocks = cells // LANES
-    assert modes * devices == MV and modes <= 8 and slabs % 2 == 0 and blocks % 4 == 0
-    half_x, half_modes = rows * slabs // 2, MX // 2
+    assert modes * devices == MV and modes <= 8 and slabs % 2 == 0 and blocks % 4 == 0 and MX % (2 * slabs) == 0
 
     table = cosine_table(cells, np.arange(MV), np.arange(cells))
     bv_high, bv_low = split_table(table)
     bvt_high, bvt_low = split_table(np.ascontiguousarray(table.T))
     packed = np.arange(rows)
     packed = PHASES * (packed % (rows // PHASES)) + packed // (rows // PHASES)
-    positions = (rows * np.arange(slabs // 2)[:, None] + packed[None, :]).reshape(-1)
-    tables_x = []
-    for parity in range(2):
-        tables_x += split_table(cosine_table(2 * half_x, 2 * np.arange(half_modes) + parity, positions))
+    ahead = residue_table(rows, slabs, packed)
+    tables_x = [twiddle_table(rows, slabs, packed), *split_table(ahead), *split_table(np.ascontiguousarray(ahead.T))]
 
     vmem = pl.BlockSpec(memory_space=pltpu.VMEM)
     smem = pl.BlockSpec(memory_space=pltpu.SMEM)
@@ -369,13 +472,17 @@
     tall = pltpu.VMEM((PHASES, cells + 2 * GUARD, LANES), F32)
     coefs = pltpu.VMEM((2, cells + 2 * GUARD, LANES), F32)
     flat = pltpu.VMEM((cells, PHASES * LANES), BF16)
-    advanced, reduced = pl.pallas_call(
-        advance_kernel,
-        out_shape=(
-            jax.ShapeDtypeStruct((PHASES, cells, LANES), F32),
-            jax.ShapeDtypeStruct((MV, rows), F32),
-        ),
-        in_specs=[smem, hbm, hbm, hbm, vmem, vmem],
+    each = parcel_rows(rows)
+
+    def exchange(parcels):
+        flat_parcels = parcels.reshape(devices, 1, each * LANES)
+        return lax.all_to_all(flat_parcels, AXES, 0, 0, tiled=True).reshape(devices * each, LANES)
+
+    parcels_shape = jax.ShapeDtypeStruct((devices * each, LANES), F32)
+    advanced, parcels = pl.pallas_call(
+        functools.partial(advance_kernel, devices=devices),
+        out_shape=(jax.ShapeDtypeStruct((PHASES, cells, LANES), F32), parcels_shape),
+        in_specs=[smem, smem, hbm, vmem, vmem, vmem, vmem],
         out_specs=(hbm, vmem),
         scratch_shapes=[
             pltpu.VMEM((blocks, PHASES * LANES, LANES), F32),
@@ -389,38 +496,21 @@
             pltpu.SemaphoreType.DMA((1,)),
         ],
         name="advance",
-    )(levels, density, above, below, bvt_high, bvt_low)
-
-    parcels = jnp.pad(reduced.reshape(devices, modes, rows), ((0, 0), (0, 8 - modes), (0, 0)))
-    parcels = lax.all_to_all(parcels, AXES, 0, 0, tiled=True)
-    note = jnp.concatenate([levels[0], coeffs])
-    note = jnp.broadcast_to(jnp.pad(note, (0, LANES - 3)), (groups, 1, LANES))
-    meta = lax.all_to_all(note, "comp", 0, 0, tiled=True).reshape(groups, LANES)
-
-    corrected, halo = pl.pallas_call(
+    )(levels, coeffs, density, above, below, bvt_high, bvt_low)
+
+    parcels = pl.pallas_call(
         functools.partial(combine_kernel, groups=groups, slabs=slabs, modes=modes),
-        out_shape=(
-            jax.ShapeDtypeStruct((devices, 8, rows), F32),
-            jax.ShapeDtypeStruct((devices, 8, LANES), F32),
-        ),
-        in_specs=[smem, vmem, hbm, hbm, hbm, hbm],
-        out_specs=(vmem, vmem),
-        scratch_shapes=[pltpu.VMEM((half_x, half_modes), BF16)] * 4
-        + [pltpu.VMEM((8 * groups, half_x), F32)] * 2
-        + [pltpu.SemaphoreType.DMA((4,))],
+        out_shape=parcels_shape,
+        in_specs=[vmem] * 6,
+        out_specs=vmem,
+        scratch_shapes=[pltpu.VMEM((8 * groups * (slabs + 1), 2 * rows), F32)],
         name="combine",
-    )(meta, parcels, *tables_x)
-
-    corrected = lax.all_to_all(corrected, AXES, 0, 0, tiled=True)
-    corrected = corrected[:, :modes].reshape(MV, rows)
-    ends = halo[:, :modes, : 2 * POST].reshape(devices, 1, modes * 2 * POST)
-    ends = lax.all_to_all(ends, AXES, 0, 0, tiled=True).reshape(MV, 2 * POST)
-    ends = jnp.pad(ends, ((0, 0), (0, LANES - 2 * POST)))
+    )(exchange(parcels), *tables_x)
 
     result = pl.pallas_call(
-        correct_kernel,
+        functools.partial(correct_kernel, devices=devices),
         out_shape=jax.ShapeDtypeStruct((rows, cells), F32),
-        in_specs=[smem, hbm, vmem, vmem, vmem, vmem],
+        in_specs=[smem, hbm, vmem, vmem, vmem],
         out_specs=hbm,
         scratch_shapes=[
             tall,
@@ -428,11 +518,13 @@
             coefs,
             pltpu.VMEM((2, PHASES, LANES, LANES), F32),
             pltpu.VMEM((blocks, rows, LANES), F32),
+            pltpu.VMEM((MV, rows), F32),
+            pltpu.VMEM((MV, LANES), F32),
             pltpu.SemaphoreType.DMA((PHASES,)),
             pltpu.SemaphoreType.DMA((1,)),
         ],
         name="correct",
-    )(levels, advanced, corrected, ends, bv_high, bv_low)
+    )(levels, advanced, exchange(parcels), bv_high, bv_low)
     return result[None]
 
 

time: 93.7 us -> 75.4 us (0.80)
  starting transfers between devices: 11.1 us -> 4.57 us
  waiting for transfers between devices: 11.7 us -> 5.53 us
  blocking collectives: 29 us -> 34.2 us
  Pallas kernels: 33.8 us -> 28.6 us
  local copies, waits for them, and re-layouts: 5.38 us -> 1.62 us
  other arithmetic: 1.45 us -> 0 us
    all_to_all x2 -> x0, waiting for transfers between devices: 11.2 us -> none  [the longest x1 11.2 us: body(): corrected = lax.all_to_all(corrected, AXES, 0, 0, tiled=True)]
    all_to_all x2 -> x0, starting transfers between devices: 6.49 us -> none  [the longest x1 3.72 us: body(): meta = lax.all_to_all(note, 'comp', 0, 0, tiled=True).reshape(groups, LANES)]
    pallas_call x1, Pallas kernels: 10.4 us -> 4.22 us  [body(): pl.pallas_call(functools.partial(combine_kernel, groups=groups, slabs=sla...]
    all_to_all x2, blocking collectives: 29 us -> 34.2 us  [exchange(): lax.all_to_all(flat_parcels, AXES, 0, 0, tiled=True)]
    ppermute x1, waiting for transfers between devices: 0.51 us -> 3.67 us  [body(): above = lax.ppermute(density[rows - HALO:], 'dom', ring)]
    ppermute x1, waiting for transfers between devices: 0.01 us -> 1.87 us  [body(): below = lax.ppermute(density[:HALO], 'dom', [(b, a) for a, b in ring])]
    slice x1 -> x0, local copies, waits for them, and re-layouts: 1.02 us -> none  [body(): ends = halo[:, :modes, :2 * POST].reshape(devices, 1, modes * 2 * POST)]
    pallas_call x2, Pallas kernels: 23.4 us -> 24.4 us  [the longest x1 15.7 us: body(): pl.pallas_call(functools.partial(advance_kernel, devices=devices), out_sh...]
  transfers between devices with their start and end apart: 4 -> 2, of which waited for: 2 -> 2; matrix products, arithmetic and copies ran while one was open for 4% -> 0% of each run, Pallas kernels for 16% -> 0%
where the time goes in v2:
time: 75.4 us; the launch traced here: 75.2 us
  blocking collectives  34.2 us (45%)
  Pallas kernels  28.6 us (38%)
  waiting for transfers between devices  5.53 us (7%)
  starting transfers between devices  4.57 us (6%)
  local copies, waits for them, and re-layouts  1.62 us (2%)
    all_to_all x2, blocking collectives, exchange(): lax.all_to_all(flat_parcels, AXES, 0, 0, tiled=True)  34.2 us
    pallas_call x1, Pallas kernels, body(): pl.pallas_call(functools.partial(advance_kernel, devices=devices), out_sh...  15.7 us
    pallas_call x1, Pallas kernels, body(): pl.pallas_call(functools.partial(correct_kernel, devices=devices), out_sh...  8.72 us
    ppermute x1, starting transfers between devices, body(): below = lax.ppermute(density[:HALO], 'dom', [(b, a) for a, b in ring])  4.57 us
    pallas_call x1, Pallas kernels, body(): pl.pallas_call(functools.partial(combine_kernel, groups=groups, slabs=sla...  4.22 us
    ppermute x1, waiting for transfers between devices, body(): above = lax.ppermute(density[rows - HALO:], 'dom', ring)  3.67 us
    ppermute x1, waiting for transfers between devices, body(): below = lax.ppermute(density[:HALO], 'dom', [(b, a) for a, b in ring])  1.87 us
  transfers between devices with their start and end apart: 2, of which 2 were waited for; matrix products, arithmetic and copies ran while one was open for 0% of the time, Pallas kernels for 0%

profile of v2, /device:TPU:0, one launch (start us, length us, event | category | flops | bytes accessed | tf_op | source)
XLA Modules:
  0.0 75.2 jit_solution(7874189854395122633)
XLA Ops:
  0.0 1.0 %slice_bitcast_fusion = (f32[16,2048]{1,0:T(8,128)S(1)}, f32[16,2048]{1,0:T(8,128)S(1)}) fusion(f32[1,384,2048]{2,1,0:T(8,128)} %param.12), kind=kLoop, calls=%fused_computation | loop fusion | bytes 524288 | tf_op jit(solution)/shard_map/slice | solution.py:469
  1.0 4.6 %collective-permute-start.1 = (f32[16,2048]{1,0:T(8,128)S(1)}, f32[16,2048]{1,0:T(8,128)S(1)}, u32[]{:S(2)}, u32[]{:S(2)}) collective-permute-start(f32[16,2048]{1,0:T(8,128)S(1)} %get-tuple-element.9), channel_id=1, source_target_pairs={{1,0},{2,1},{3,2},{4,3},{5,4},{6,5},{7,6},{0,7},{9,8},{10,9},{11,1... | collective-permute-start | bytes 393224 | tf_op jit(solution)/shard_map/ppermute | solution.py:469
  5.6 0.0 collective-permute-start
  6.2 1.9 %collective-permute-done.1.below = f32[16,2048]{1,0:T(8,128)S(1)} collective-permute-done((f32[16,2048]{1,0:T(8,128)S(1)}, f32[16,2048]{1,0:T(8,128)S(1)}, u32[]{:S(2)}, u32[]{:S(2)}) %collective-permute-start.1) | collective-permute-done | bytes 131104 | tf_op jit(solution)/shard_map/ppermute | solution.py:469
  8.1 0.0 copy-start
  8.1 3.7 %collective-permute-done.above = f32[16,2048]{1,0:T(8,128)S(1)} collective-permute-done((f32[16,2048]{1,0:T(8,128)S(1)}, f32[16,2048]{1,0:T(8,128)S(1)}, u32[]{:S(2)}, u32[]{:S(2)}) %collective-permute-start) | collective-permute-done | bytes 131104 | tf_op jit(solution)/shard_map/ppermute | solution.py:468
  11.8 0.0 copy-start.1
  11.8 0.0 copy-done
  11.8 0.6 copy-done.1
  12.4 15.7 %advance.1 = (f32[4,2048,128]{2,1,0:T(8,128)}, f32[800,128]{1,0:T(8,128)}) custom-call(s32[1,2]{1,0:T(1,128)} %levels.3, s32[1]{0:T(128)S(6)} %copy.15.coeffs, f32[384,2048]{1,0:T(8,128)} %bitcast.10, f32[16,2048]{1,0:T(8,128)} %copy-done.1, f32[16,2048]{1,0:T(8,128)} %copy-done, bf16[256,2048]{1,0:T(8,128)(2,1)} %constant.18.clone.bvt_high, ...), custom_call_target="tpu_custom_call" | custom-call | tf_op jit(solution)/shard_map/advance/pallas_call | solution.py:482
  28.1 17.1 %all_to_all.10 = f32[32,1,3200]{2,1,0:T(1,128)} all-to-all(f32[32,1,3200]{2,1,0:T(1,128)} %bitcast.14), channel_id=1, replica_groups=mesh['comp'=4,'dom'=8] {'comp','dom'}, dimensions={0} | all-to-all | bytes 819200 | tf_op jit(solution)/shard_map/all_to_all | solution.py:479
  45.2 4.2 %combine.1 = f32[800,128]{1,0:T(8,128)} custom-call(f32[800,128]{1,0:T(8,128)} %bitcast.11, f32[2,9,1,384]{3,2,1,0:T(1,128)} %constant.20.clone.twiddle, bf16[768,256]{1,0:T(8,128)(2,1)} %constant.21.clone.ahead_high, bf16[768,256]{1,0:T(8,128)(2,1)} %constant.22.clone.ahead_low, bf16[256,768]{1,0:T(8,128)(2,1)} %constant.23.clone.back_high, ...), custom_call_target="tpu_custom_call" | custom-call | tf_op jit(solution)/shard_map/combine/pallas_call | solution.py:501
  49.4 17.1 %all_to_all.11 = f32[32,1,3200]{2,1,0:T(1,128)} all-to-all(f32[32,1,3200]{2,1,0:T(1,128)} %bitcast.12), channel_id=1, replica_groups=mesh['comp'=4,'dom'=8] {'comp','dom'}, dimensions={0} | all-to-all | bytes 819200 | tf_op jit(solution)/shard_map/all_to_all | solution.py:479
  66.5 8.7 %correct.1 = f32[384,2048]{1,0:T(8,128)} custom-call(s32[1,2]{1,0:T(1,128)} %levels.3, f32[4,2048,128]{2,1,0:T(8,128)} %get-tuple-element.7.advanced, f32[800,128]{1,0:T(8,128)} %bitcast.13, bf16[2048,256]{1,0:T(8,128)(2,1)} %constant.25.clone.bv_high, bf16[2048,256]{1,0:T(8,128)(2,1)} %constant.26.clone.bv_low), custom_call_target="tpu_custom_call" | custom-call | tf_op jit(solution)/shard_map/correct/pallas_call | solution.py:510
Async XLA Ops:
  1.0 7.1 %collective-permute-start.1 = (f32[16,2048]{1,0:T(8,128)S(1)}, f32[16,2048]{1,0:T(8,128)S(1)}, u32[]{:S(2)}, u32[]{:S(2)}) collective-permute-start(f32[16,2048]{1,0:T(8,128)S(1)} %get-tuple-element.9), channel_id=1, source_target_pairs={{1,0},{2,1},{3,2},{4,3},{5,4},{6,5},{7,6},{0,7},{9,8},{10,9},{11,1... | collective-permute-start | bytes 393224 | tf_op jit(solution)/shard_map/ppermute | solution.py:469
  5.6 6.2 %collective-permute-start = (f32[16,2048]{1,0:T(8,128)S(1)}, f32[16,2048]{1,0:T(8,128)S(1)}, u32[]{:S(2)}, u32[]{:S(2)}) collective-permute-start(f32[16,2048]{1,0:T(8,128)S(1)} %get-tuple-element.10), channel_id=1, source_target_pairs={{0,1},{1,2},{2,3},{3,4},{4,5},{5,6},{6,7},{7,0},{8,9},{9,10},{10,1... | collective-permute-start | bytes 393224 | tf_op jit(solution)/shard_map/ppermute | solution.py:468
  8.1 3.7 %copy-start = (f32[16,2048]{1,0:T(8,128)}, f32[16,2048]{1,0:T(8,128)S(1)}, u32[]{:S(2)}) copy-start(f32[16,2048]{1,0:T(8,128)S(1)} %collective-permute-done.1.below) | copy-start | bytes 393220
  11.8 0.6 copy-start.1

commit v3 on v2

--- a/solution.py
+++ b/solution.py
@@ -18,6 +18,7 @@
 PHASES = 4
 MARGIN = 8
 GUARD = 8
+VMEM_LIMIT = 32 * 2**20
 AXES = ("comp", "dom")
 F32 = jnp.float32
 BF16 = jnp.bfloat16
@@ -137,8 +138,8 @@
 
 
 def advance_kernel(
-    levels, coeffs, cells, above, below, bvt_high, bvt_low, advanced, parcels,
-    natural, first, second, third, coef, high, low, fetches, sems, *, devices,
+    levels, coeffs, cells, above, below, bvt_high_hbm, bvt_low_hbm, advanced, parcels,
+    natural, first, second, coef, high, low, bvt_high, bvt_low, fetches, sems, *, devices,
 ):
     rows, width = cells.shape
     planes = width // LANES
@@ -150,6 +151,12 @@
             pltpu.make_async_copy(cells.at[:, lanes], natural.at[c, pl.ds(start, rows), :], fetches.at[c])
         )
         fetched[c].start()
+    tables = [
+        pltpu.make_async_copy(bvt_high_hbm, bvt_high, sems.at[0]),
+        pltpu.make_async_copy(bvt_low_hbm, bvt_low, sems.at[1]),
+    ]
+    for copy in tables:
+        copy.start()
     level_x, courant, diffusion = rates(levels)
     count = jnp.clip(PRE - 3 + level_x, 0, PRE)
     scale = lax.fori_loop(0, count, lambda i, s: s * diffusion, jnp.float32(1.0))
@@ -184,7 +191,7 @@
                     row = pl.multiple_of(begin + (i * unroll + k) * 16, 16)
                     for t, value in enumerate(stepped(src, coef, GUARD + row, 16, leftward)):
                         value = value * scale
-                        third[t, pl.ds(row, 16), :] = value
+                        advanced[t, pl.ds(row, 16), :] = value
                         lanes = pl.ds(t * LANES, LANES)
                         high[pl.ds(row, 16), lanes], low[pl.ds(row, 16), lanes] = split(value)
                 return carry
@@ -200,8 +207,8 @@
     def _():
         final(first)
 
-    out = pltpu.make_async_copy(third, advanced, sems.at[0])
-    out.start()
+    for copy in tables:
+        copy.wait()
     total = dot(bvt_high[...], high[...]) + dot(bvt_low[...], high[...]) + dot(bvt_high[...], low[...])
     modes = bvt_high.shape[0] // devices
     lane = lax.broadcasted_iota(jnp.int32, (1, LANES), 1)
@@ -219,7 +226,6 @@
             parcels[pl.ds(parcel_rows(rows) * q + 8 * j, modes), :] = packed[modes * q : modes * (q + 1)]
     for q in range(devices):
         parcels[pl.ds(parcel_rows(rows) * (q + 1) - 1, 1), :] = note
-    out.wait()
 
 
 def rotate_sums(terms):
@@ -383,15 +389,10 @@
 
 def correct_kernel(
     levels, advanced, parcels, bv_high, bv_low, result, first, second, coef, work, natural, corrected, halo,
-    fetches, sems, *, devices,
+    sems, *, devices,
 ):
     rows, width = result.shape
     planes = width // LANES
-    fetched = [
-        pltpu.make_async_copy(advanced.at[t], first.at[t, pl.ds(GUARD, width), :], fetches.at[t]) for t in range(PHASES)
-    ]
-    for copy in fetched:
-        copy.start()
     _, courant, diffusion = rates(levels)
     fill_coefs(coef, width, courant, diffusion)
     scale = jnp.float32(1.0)
@@ -416,15 +417,13 @@
                 pieces.append((halo[...], h, (x + PHASES * MARGIN) // PHASES, 1))
         wide.append(moved_lanes(pieces))
     high, low = split(jnp.concatenate(wide, axis=1))
-    for copy in fetched:
-        copy.wait()
     size = 2 * LANES
     for i in range(width // size):
         where = pl.ds(i * size, size)
         left_high, left_low = bv_high[where, :], bv_low[where, :]
         change = dot(left_high, high) + dot(left_high, low) + dot(left_low, high)
         for t in range(PHASES):
-            first[t, pl.ds(GUARD + i * size, size), :] += change[:, t * LANES : (t + 1) * LANES]
+            first[t, pl.ds(GUARD + i * size, size), :] = advanced[t, where, :] + change[:, t * LANES : (t + 1) * LANES]
     mirror_edges(first, width)
     source, other = first, second
     for _ in range(POST - 1):
@@ -444,6 +443,14 @@
         copy.wait()
 
 
+def in_vmem(value):
+    return pltpu.with_memory_space_constraint(value, pltpu.VMEM)
+
+
+def in_hbm(value):
+    return pltpu.with_memory_space_constraint(value, pltpu.HBM)
+
+
 def body(densities, levels, coeffs):
     density = densities[0]
     rows, cells = density.shape
@@ -465,8 +472,8 @@
     smem = pl.BlockSpec(memory_space=pltpu.SMEM)
     hbm = pl.BlockSpec(memory_space=pl.ANY)
     ring = [(i, (i + 1) % slabs) for i in range(slabs)]
-    above = lax.ppermute(density[rows - HALO :], "dom", ring)
-    below = lax.ppermute(density[:HALO], "dom", [(b, a) for a, b in ring])
+    above = in_vmem(lax.ppermute(density[rows - HALO :], "dom", ring))
+    below = in_vmem(lax.ppermute(density[:HALO], "dom", [(b, a) for a, b in ring]))
 
     assert rows % LANES == 0 and rows + HALO <= PHASES * (LANES - MARGIN) and PRE + POST <= HALO
     tall = pltpu.VMEM((PHASES, cells + 2 * GUARD, LANES), F32)
@@ -476,27 +483,29 @@
 
     def exchange(parcels):
         flat_parcels = parcels.reshape(devices, 1, each * LANES)
-        return lax.all_to_all(flat_parcels, AXES, 0, 0, tiled=True).reshape(devices * each, LANES)
-
-    parcels_shape = jax.ShapeDtypeStruct((devices * each, LANES), F32)
+        return in_vmem(lax.all_to_all(flat_parcels, AXES, 0, 0, tiled=True).reshape(devices * each, LANES))
+
+    parcels_shape = pltpu.VMEM((devices * each, LANES), F32)
     advanced, parcels = pl.pallas_call(
         functools.partial(advance_kernel, devices=devices),
-        out_shape=(jax.ShapeDtypeStruct((PHASES, cells, LANES), F32), parcels_shape),
-        in_specs=[smem, smem, hbm, vmem, vmem, vmem, vmem],
-        out_specs=(hbm, vmem),
+        out_shape=(pltpu.VMEM((PHASES, cells, LANES), F32), parcels_shape),
+        in_specs=[smem, smem, hbm, vmem, vmem, hbm, hbm],
+        out_specs=(vmem, vmem),
         scratch_shapes=[
             pltpu.VMEM((blocks, PHASES * LANES, LANES), F32),
             tall,
             tall,
-            pltpu.VMEM((PHASES, cells, LANES), F32),
             coefs,
             flat,
             flat,
+            pltpu.VMEM((MV, cells), BF16),
+            pltpu.VMEM((MV, cells), BF16),
             pltpu.SemaphoreType.DMA((blocks,)),
-            pltpu.SemaphoreType.DMA((1,)),
+            pltpu.SemaphoreType.DMA((2,)),
         ],
+        compiler_params=pltpu.CompilerParams(vmem_limit_bytes=VMEM_LIMIT),
         name="advance",
-    )(levels, coeffs, density, above, below, bvt_high, bvt_low)
+    )(in_hbm(levels), coeffs, in_hbm(density), above, below, in_hbm(bvt_high), in_hbm(bvt_low))
 
     parcels = pl.pallas_call(
         functools.partial(combine_kernel, groups=groups, slabs=slabs, modes=modes),
@@ -504,13 +513,14 @@
         in_specs=[vmem] * 6,
         out_specs=vmem,
         scratch_shapes=[pltpu.VMEM((8 * groups * (slabs + 1), 2 * rows), F32)],
+        compiler_params=pltpu.CompilerParams(vmem_limit_bytes=VMEM_LIMIT),
         name="combine",
-    )(exchange(parcels), *tables_x)
+    )(exchange(parcels), *map(in_vmem, tables_x))
 
     result = pl.pallas_call(
         functools.partial(correct_kernel, devices=devices),
         out_shape=jax.ShapeDtypeStruct((rows, cells), F32),
-        in_specs=[smem, hbm, vmem, vmem, vmem],
+        in_specs=[smem, vmem, vmem, vmem, vmem],
         out_specs=hbm,
         scratch_shapes=[
             tall,
@@ -520,11 +530,11 @@
             pltpu.VMEM((blocks, rows, LANES), F32),
             pltpu.VMEM((MV, rows), F32),
             pltpu.VMEM((MV, LANES), F32),
-            pltpu.SemaphoreType.DMA((PHASES,)),
             pltpu.SemaphoreType.DMA((1,)),
         ],
+        compiler_params=pltpu.CompilerParams(vmem_limit_bytes=VMEM_LIMIT),
         name="correct",
-    )(levels, advanced, exchange(parcels), bv_high, bv_low)
+    )(in_hbm(levels), advanced, exchange(parcels), in_vmem(bv_high), in_vmem(bv_low))
     return result[None]
 
 

time: 75.4 us -> 66.1 us (0.88)
  Pallas kernels: 28.6 us -> 22.6 us
  blocking collectives: 34.2 us -> 31.4 us
    all_to_all x2, blocking collectives: 34.2 us -> 31.4 us  [exchange(): lax.all_to_all(flat_parcels, AXES, 0, 0, tiled=True)]
    pallas_call x1, Pallas kernels: 4.22 us -> 2 us  [body(): pl.pallas_call(functools.partial(combine_kernel, groups=groups, slabs=sla...]
    pallas_call x1, Pallas kernels: 8.72 us -> 6.54 us  [body(): pl.pallas_call(functools.partial(correct_kernel, devices=devices), out_sh...]
    pallas_call x1, Pallas kernels: 15.7 us -> 14.1 us  [body(): pl.pallas_call(functools.partial(advance_kernel, devices=devices), out_sh...]
where the time goes in v3:
time: 66.1 us; the launch traced here: 65.9 us
  blocking collectives  31.4 us (48%)
  Pallas kernels  22.6 us (34%)
  waiting for transfers between devices  5.54 us (8%)
  starting transfers between devices  4.57 us (7%)
  local copies, waits for them, and re-layouts  1.02 us (2%)
  between operations  0.72 us (1%)
    all_to_all x2, blocking collectives, exchange(): lax.all_to_all(flat_parcels, AXES, 0, 0, tiled=True)  31.4 us
    pallas_call x1, Pallas kernels, body(): pl.pallas_call(functools.partial(advance_kernel, devices=devices), out_sh...  14.1 us
    pallas_call x1, Pallas kernels, body(): pl.pallas_call(functools.partial(correct_kernel, devices=devices), out_sh...  6.54 us
    ppermute x1, starting transfers between devices, body(): lax.ppermute(density[:HALO], 'dom', [(b, a) for a, b in ring])  4.57 us
    ppermute x1, waiting for transfers between devices, body(): above = in_vmem(lax.ppermute(density[rows - HALO:], 'dom', ring))  3.67 us
    pallas_call x1, Pallas kernels, body(): pl.pallas_call(functools.partial(combine_kernel, groups=groups, slabs=sla...  2 us
    ppermute x1, waiting for transfers between devices, body(): lax.ppermute(density[:HALO], 'dom', [(b, a) for a, b in ring])  1.87 us
  transfers between devices with their start and end apart: 2, of which 2 were waited for; matrix products, arithmetic and copies ran while one was open for 0% of the time, Pallas kernels for 0%

profile of v3, /device:TPU:0, one launch (start us, length us, event | category | flops | bytes accessed | tf_op | source)
XLA Modules:
  0.0 65.9 jit_solution(16052078744173497589)
XLA Ops:
  0.0 1.0 %slice_bitcast_fusion = (f32[16,2048]{1,0:T(8,128)S(1)}, f32[16,2048]{1,0:T(8,128)S(1)}) fusion(f32[1,384,2048]{2,1,0:T(8,128)} %param.12), kind=kLoop, calls=%fused_computation | loop fusion | bytes 524288 | tf_op jit(solution)/shard_map/slice | solution.py:476
  1.0 4.6 %collective-permute-start.1 = (f32[16,2048]{1,0:T(8,128)S(1)}, f32[16,2048]{1,0:T(8,128)S(1)}, u32[]{:S(2)}, u32[]{:S(2)}) collective-permute-start(f32[16,2048]{1,0:T(8,128)S(1)} %get-tuple-element.9), channel_id=1, source_target_pairs={{1,0},{2,1},{3,2},{4,3},{5,4},{6,5},{7,6},{0,7},{9,8},{10,9},{11,1... | collective-permute-start | bytes 393224 | tf_op jit(solution)/shard_map/ppermute | solution.py:476
  5.6 0.0 collective-permute-start
  6.2 1.9 %collective-permute-done.1.below = f32[16,2048]{1,0:T(8,128)S(1)} collective-permute-done((f32[16,2048]{1,0:T(8,128)S(1)}, f32[16,2048]{1,0:T(8,128)S(1)}, u32[]{:S(2)}, u32[]{:S(2)}) %collective-permute-start.1) | collective-permute-done | bytes 131104 | tf_op jit(solution)/shard_map/ppermute | solution.py:476
  8.1 3.7 %collective-permute-done.above = f32[16,2048]{1,0:T(8,128)S(1)} collective-permute-done((f32[16,2048]{1,0:T(8,128)S(1)}, f32[16,2048]{1,0:T(8,128)S(1)}, u32[]{:S(2)}, u32[]{:S(2)}) %collective-permute-start) | collective-permute-done | bytes 131104 | tf_op jit(solution)/shard_map/ppermute | solution.py:475
  11.8 0.0 copy-start.2
  11.8 0.0 copy-start.3
  11.8 0.0 copy-start.4
  11.8 0.0 copy-start.5
  11.8 0.0 copy-start.6
  11.8 14.1 %advance.1 = (f32[4,2048,128]{2,1,0:T(8,128)S(1)}, f32[800,128]{1,0:T(8,128)S(1)}) custom-call(s32[1,2]{1,0:T(1,128)} %levels.3, s32[1]{0:T(128)S(6)} %copy.15.coeffs, f32[384,2048]{1,0:T(8,128)} %bitcast.14, f32[16,2048]{1,0:T(8,128)S(1)} %collective-permute-done.above, f32[16,2048]{1,0:T(8,128)S(1)} %collective-permute-done.1.below, ...), custom_call_target="tpu_custom_call" | custom-call | tf_op jit(solution)/shard_map/advance/pallas_call | solution.py:489
  25.9 0.0 copy-start
  25.9 0.0 copy-start.1
  25.9 15.6 %all_to_all.10 = f32[32,1,3200]{2,1,0:T(1,128)S(1)} all-to-all(f32[32,1,3200]{2,1,0:T(1,128)S(1)} %bitcast.13), channel_id=1, replica_groups=mesh['comp'=4,'dom'=8] {'comp','dom'}, dimensions={0} | all-to-all | bytes 819200 | tf_op jit(solution)/shard_map/all_to_all | solution.py:486
  41.5 0.0 copy-done.2
  41.5 0.0 copy-done.3
  41.5 0.0 copy-done.4
  41.5 0.0 copy-done.5
  41.5 0.0 copy-done.6
  41.5 2.0 %combine.1 = f32[800,128]{1,0:T(8,128)S(1)} custom-call(f32[800,128]{1,0:T(8,128)S(1)} %bitcast.10, f32[2,9,1,384]{3,2,1,0:T(1,128)S(1)} %copy-done.6, bf16[768,256]{1,0:T(8,128)(2,1)S(1)} %copy-done.5, bf16[768,256]{1,0:T(8,128)(2,1)S(1)} %copy-done.4, bf16[256,768]{1,0:T(8,128)(2,1)S(1)} %copy-done.3, bf16[256,768]{1,0:T(8,128)(2,1)S(1)} %copy-done.2), custom_call_target="tpu_custom_call" | custom-call | tf_op jit(solution)/shard_map/combine/pallas_call | solution.py:510
  43.5 15.8 %all_to_all.11 = f32[32,1,3200]{2,1,0:T(1,128)S(1)} all-to-all(f32[32,1,3200]{2,1,0:T(1,128)S(1)} %bitcast.11), channel_id=1, replica_groups=mesh['comp'=4,'dom'=8] {'comp','dom'}, dimensions={0} | all-to-all | bytes 819200 | tf_op jit(solution)/shard_map/all_to_all | solution.py:486
  59.3 0.0 copy-done
  59.3 0.0 copy-done.1
  59.3 6.5 %correct.1 = f32[384,2048]{1,0:T(8,128)} custom-call(s32[1,2]{1,0:T(1,128)} %levels.3, f32[4,2048,128]{2,1,0:T(8,128)S(1)} %get-tuple-element.7.advanced, f32[800,128]{1,0:T(8,128)S(1)} %bitcast.12, bf16[2048,256]{1,0:T(8,128)(2,1)S(1)} %copy-done.1, bf16[2048,256]{1,0:T(8,128)(2,1)S(1)} %copy-done), custom_call_target="tpu_custom_call" | custom-call | tf_op jit(solution)/shard_map/correct/pallas_call | solution.py:520
Async XLA Ops:
  1.0 7.1 %collective-permute-start.1 = (f32[16,2048]{1,0:T(8,128)S(1)}, f32[16,2048]{1,0:T(8,128)S(1)}, u32[]{:S(2)}, u32[]{:S(2)}) collective-permute-start(f32[16,2048]{1,0:T(8,128)S(1)} %get-tuple-element.9), channel_id=1, source_target_pairs={{1,0},{2,1},{3,2},{4,3},{5,4},{6,5},{7,6},{0,7},{9,8},{10,9},{11,1... | collective-permute-start | bytes 393224 | tf_op jit(solution)/shard_map/ppermute | solution.py:476
  5.6 6.2 %collective-permute-start = (f32[16,2048]{1,0:T(8,128)S(1)}, f32[16,2048]{1,0:T(8,128)S(1)}, u32[]{:S(2)}, u32[]{:S(2)}) collective-permute-start(f32[16,2048]{1,0:T(8,128)S(1)} %get-tuple-element.10), channel_id=1, source_target_pairs={{0,1},{1,2},{2,3},{3,4},{4,5},{5,6},{6,7},{7,0},{8,9},{9,10},{10,1... | collective-permute-start | bytes 393224 | tf_op jit(solution)/shard_map/ppermute | solution.py:475
  11.8 29.8 %copy-start.2 = (bf16[256,768]{1,0:T(8,128)(2,1)S(1)}, bf16[256,768]{1,0:T(8,128)(2,1)}, u32[]{:S(2)}) copy-start(bf16[256,768]{1,0:T(8,128)(2,1)} %constant.24.clone.back_low) | copy-start | bytes 1179652
  11.8 29.8 %copy-start.3 = (bf16[256,768]{1,0:T(8,128)(2,1)S(1)}, bf16[256,768]{1,0:T(8,128)(2,1)}, u32[]{:S(2)}) copy-start(bf16[256,768]{1,0:T(8,128)(2,1)} %constant.23.clone.back_high) | copy-start | bytes 1179652
  11.8 29.8 %copy-start.4 = (bf16[768,256]{1,0:T(8,128)(2,1)S(1)}, bf16[768,256]{1,0:T(8,128)(2,1)}, u32[]{:S(2)}) copy-start(bf16[768,256]{1,0:T(8,128)(2,1)} %constant.22.clone.ahead_low) | copy-start | bytes 1179652
  11.8 29.8 %copy-start.5 = (bf16[768,256]{1,0:T(8,128)(2,1)S(1)}, bf16[768,256]{1,0:T(8,128)(2,1)}, u32[]{:S(2)}) copy-start(bf16[768,256]{1,0:T(8,128)(2,1)} %constant.21.clone.ahead_high) | copy-start | bytes 1179652
  11.8 29.8 %copy-start.6 = (f32[2,9,1,384]{3,2,1,0:T(1,128)S(1)}, f32[2,9,1,384]{3,2,1,0:T(1,128)}, u32[]{:S(2)}) copy-start(f32[2,9,1,384]{3,2,1,0:T(1,128)} %constant.20.clone.twiddle) | copy-start | bytes 82948
  25.9 33.5 %copy-start = (bf16[2048,256]{1,0:T(8,128)(2,1)S(1)}, bf16[2048,256]{1,0:T(8,128)(2,1)}, u32[]{:S(2)}) copy-start(bf16[2048,256]{1,0:T(8,128)(2,1)} %constant.26.clone.bv_low) | copy-start | bytes 3145732
  25.9 33.5 %copy-start.1 = (bf16[2048,256]{1,0:T(8,128)(2,1)S(1)}, bf16[2048,256]{1,0:T(8,128)(2,1)}, u32[]{:S(2)}) copy-start(bf16[2048,256]{1,0:T(8,128)(2,1)} %constant.25.clone.bv_high) | copy-start | bytes 3145732

commit v4 on v3

--- a/solution.py
+++ b/solution.py
@@ -137,42 +137,76 @@
     return (x % PHASES) * (rows // PHASES) + x // PHASES
 
 
-def advance_kernel(
-    levels, coeffs, cells, above, below, bvt_high_hbm, bvt_low_hbm, advanced, parcels,
-    natural, first, second, coef, high, low, bvt_high, bvt_low, fetches, sems, *, devices,
-):
+def turn_kernel(levels, cells, turned, coef, natural, fetches):
     rows, width = cells.shape
-    planes = width // LANES
     start = PHASES * MARGIN
-    fetched = []
-    for c in range(planes):
+    tail = start + rows
+    copies = []
+    for c in range(width // LANES):
         lanes = pl.ds(c * LANES, LANES)
-        fetched.append(
+        copies.append(
             pltpu.make_async_copy(cells.at[:, lanes], natural.at[c, pl.ds(start, rows), :], fetches.at[c])
         )
-        fetched[c].start()
+        copies[c].start()
+    _, courant, diffusion = rates(levels)
+    fill_coefs(coef, width, courant, diffusion)
+    for c, copy in enumerate(copies):
+        natural[c, pl.ds(0, start), :] = jnp.zeros((start, LANES), F32)
+        natural[c, pl.ds(tail, PHASES * LANES - tail), :] = jnp.zeros((PHASES * LANES - tail, LANES), F32)
+        copy.wait()
+        for t in range(PHASES):
+            turned[t, pl.ds(c * LANES, LANES), :] = natural[c, pl.ds(t, LANES, stride=PHASES), :].T
+
+
+def advance_kernel(
+    levels, coeffs, turned, coef, above, below, bvt_high_hbm, bvt_low_hbm, advanced, parcels,
+    first, second, halos, strips, high, low, bvt_high, bvt_low, sems, *, devices, rows,
+):
+    width = turned.shape[1]
+    planes = width // LANES
     tables = [
         pltpu.make_async_copy(bvt_high_hbm, bvt_high, sems.at[0]),
         pltpu.make_async_copy(bvt_low_hbm, bvt_low, sems.at[1]),
     ]
     for copy in tables:
         copy.start()
-    level_x, courant, diffusion = rates(levels)
+    level_x, _, diffusion = rates(levels)
     count = jnp.clip(PRE - 3 + level_x, 0, PRE)
     scale = lax.fori_loop(0, count, lambda i, s: s * diffusion, jnp.float32(1.0))
-    fill_coefs(coef, width, courant, diffusion)
-    top, tail = start - HALO, start + rows + HALO
-    for c in range(planes):
-        natural[c, pl.ds(0, top), :] = jnp.zeros((top, LANES), F32)
-        natural[c, pl.ds(tail, PHASES * LANES - tail), :] = jnp.zeros((PHASES * LANES - tail, LANES), F32)
-        lanes = pl.ds(c * LANES, LANES)
-        natural[c, pl.ds(top, HALO), :] = above[:, lanes]
-        natural[c, pl.ds(start + rows, HALO), :] = below[:, lanes]
-        fetched[c].wait()
-        for t in range(PHASES):
-            first[t, pl.ds(GUARD + c * LANES, LANES), :] = natural[c, pl.ds(t, LANES, stride=PHASES), :].T
-    mirror_edges(first, width)
+    run = HALO // PHASES
+    sides = ((MARGIN - run, 0), (MARGIN + rows // PHASES, HALO))
+    shift = 2 * run
+    lane = lax.broadcasted_iota(jnp.int32, (LANES, LANES), 1)
+    is_halo = jnp.zeros((LANES, LANES), jnp.bool_)
+    for low_lane, _ in sides:
+        is_halo = is_halo | ((lane >= low_lane) & (lane < low_lane + run))
+
+    def insert(target):
+        for c in range(planes):
+            lanes = pl.ds(c * LANES, LANES)
+            halos[c, pl.ds(0, HALO), :] = above[:, lanes]
+            halos[c, pl.ds(HALO, HALO), :] = below[:, lanes]
+            for t in range(PHASES):
+                for low_lane, row in sides:
+                    at = (low_lane + shift * t) % LANES
+                    strips[c, pl.ds(at, run), :] = halos[c, pl.ds(row + t, run, stride=PHASES), :]
+            strip = strips[c].T
+            where = pl.ds(c * LANES, LANES)
+            for t in range(PHASES):
+                moved = pltpu.roll(strip, LANES - shift * t, axis=1) if t else strip
+                target[t, pl.ds(GUARD + c * LANES, LANES), :] = jnp.where(is_halo, moved, turned[t, where, :])
+        mirror_edges(target, width)
+
     inner = count - 1
+
+    @pl.when(inner % 2 == 0)
+    def _():
+        insert(first)
+
+    @pl.when(inner % 2 == 1)
+    def _():
+        insert(second)
+        inner_step(second, first, coef, width)
 
     def pair(i, carry):
         inner_step(first, second, coef, width)
@@ -180,36 +214,25 @@
         return carry
 
     lax.fori_loop(0, inner // 2, pair, 0)
-
-    def final(src):
-        unroll = 16
-        for leftward in (True, False):
-            begin = 0 if leftward else width // 2
-
-            def body(i, carry):
-                for k in range(unroll):
-                    row = pl.multiple_of(begin + (i * unroll + k) * 16, 16)
-                    for t, value in enumerate(stepped(src, coef, GUARD + row, 16, leftward)):
-                        value = value * scale
-                        advanced[t, pl.ds(row, 16), :] = value
-                        lanes = pl.ds(t * LANES, LANES)
-                        high[pl.ds(row, 16), lanes], low[pl.ds(row, 16), lanes] = split(value)
-                return carry
-
-            lax.fori_loop(0, width // 32 // unroll, body, 0)
-
-    @pl.when(inner % 2 == 1)
-    def _():
-        inner_step(first, second, coef, width)
-        final(second)
-
-    @pl.when(inner % 2 == 0)
-    def _():
-        final(first)
-
     for copy in tables:
         copy.wait()
-    total = dot(bvt_high[...], high[...]) + dot(bvt_low[...], high[...]) + dot(bvt_high[...], low[...])
+    size = 2 * LANES
+    total = None
+    for i in range(width // size + 1):
+        if i < width // size:
+            for k in range(size // 16):
+                row = i * size + k * 16
+                for t, value in enumerate(stepped(first, coef, GUARD + row, 16, row < width // 2)):
+                    value = value * scale
+                    advanced[t, pl.ds(row, 16), :] = value
+                    lanes = pl.ds(t * LANES, LANES)
+                    high[pl.ds(row, 16), lanes], low[pl.ds(row, 16), lanes] = split(value)
+        if i > 0:
+            where = pl.ds((i - 1) * size, size)
+            left_high, left_low = bvt_high[:, where], bvt_low[:, where]
+            right_high, right_low = high[where, :], low[where, :]
+            part = dot(left_high, right_high) + dot(left_low, right_high) + dot(left_high, right_low)
+            total = part if total is None else total + part
     modes = bvt_high.shape[0] // devices
     lane = lax.broadcasted_iota(jnp.int32, (1, LANES), 1)
     note = jnp.where(lane == 0, (1 << (3 - level_x)).astype(F32) / MX, 0.0)
@@ -388,16 +411,11 @@
 
 
 def correct_kernel(
-    levels, advanced, parcels, bv_high, bv_low, result, first, second, coef, work, natural, corrected, halo,
-    sems, *, devices,
+    levels, advanced, coef, parcels, bv_high, bv_low, result, first, second, work, natural, corrected, halo, sems, *, devices
 ):
     rows, width = result.shape
     planes = width // LANES
-    _, courant, diffusion = rates(levels)
-    fill_coefs(coef, width, courant, diffusion)
-    scale = jnp.float32(1.0)
-    for _ in range(POST):
-        scale = scale * diffusion
+    _, _, diffusion = rates(levels)
     each, modes = parcel_rows(rows), bv_high.shape[1] // devices
     for q in range(devices):
         where = pl.ds(modes * q, modes)
@@ -418,27 +436,53 @@
         wide.append(moved_lanes(pieces))
     high, low = split(jnp.concatenate(wide, axis=1))
     size = 2 * LANES
-    for i in range(width // size):
-        where = pl.ds(i * size, size)
-        left_high, left_low = bv_high[where, :], bv_low[where, :]
-        change = dot(left_high, high) + dot(left_high, low) + dot(left_low, high)
-        for t in range(PHASES):
-            first[t, pl.ds(GUARD + i * size, size), :] = advanced[t, where, :] + change[:, t * LANES : (t + 1) * LANES]
-    mirror_edges(first, width)
-    source, other = first, second
-    for _ in range(POST - 1):
-        inner_step(source, other, coef, width)
-        source, other = other, source
+    chunks = width // size
+    scale = diffusion * diffusion
+    assert POST == 2
     copies = []
-    for c in range(planes):
-        for k in range(LANES // 8):
-            for t, value in enumerate(stepped(source, coef, GUARD + c * LANES + 8 * k, 8, c < planes // 2)):
-                work[c % 2, t, pl.ds(8 * k, 8), :] = value * scale
-        for t in range(PHASES):
-            back = work[c % 2, t].T
-            natural[c, pl.ds(t, rows // PHASES, stride=PHASES), :] = back[MARGIN : MARGIN + rows // PHASES]
-        copies.append(pltpu.make_async_copy(natural.at[c], result.at[:, pl.ds(c * LANES, LANES)], sems.at[0]))
-        copies[-1].start()
+    stepped_to, plane = 0, 0
+    for i in range(chunks + 2):
+        if i > 1:
+            ready = planes if i == chunks + 1 else (stepped_to - 1) // LANES
+            while plane < ready:
+                c = plane
+                for k in range(LANES // 8):
+                    values = stepped(second, coef, GUARD + c * LANES + 8 * k, 8, c < planes // 2)
+                    for t, value in enumerate(values):
+                        work[c % 2, t, pl.ds(8 * k, 8), :] = value * scale
+                for t in range(PHASES):
+                    back = work[c % 2, t].T
+                    natural[c, pl.ds(t, rows // PHASES, stride=PHASES), :] = back[MARGIN : MARGIN + rows // PHASES]
+                copies.append(
+                    pltpu.make_async_copy(natural.at[c], result.at[:, pl.ds(c * LANES, LANES)], sems.at[0])
+                )
+                copies[-1].start()
+                plane += 1
+        if 0 < i <= chunks:
+            if i == chunks:
+                for t in range(PHASES):
+                    first[t, pl.ds(GUARD + width, 1), :] = first[t, pl.ds(GUARD + width - 1, 1), :]
+            last = width if i == chunks else i * size - 8
+            for row in range(stepped_to, last, 8):
+                for t, value in enumerate(stepped(first, coef, GUARD + row, 8, row < width // 2)):
+                    second[t, pl.ds(GUARD + row, 8), :] = value
+            if i == 1:
+                for t in range(PHASES):
+                    second[t, pl.ds(GUARD - 1, 1), :] = second[t, pl.ds(GUARD, 1), :]
+            if i == chunks:
+                for t in range(PHASES):
+                    second[t, pl.ds(GUARD + width, 1), :] = second[t, pl.ds(GUARD + width - 1, 1), :]
+            stepped_to = last
+        if i < chunks:
+            where = pl.ds(i * size, size)
+            left_high, left_low = bv_high[where, :], bv_low[where, :]
+            change = dot(left_high, high) + dot(left_high, low) + dot(left_low, high)
+            for t in range(PHASES):
+                lanes = slice(t * LANES, (t + 1) * LANES)
+                first[t, pl.ds(GUARD + i * size, size), :] = advanced[t, where, :] + change[:, lanes]
+            if i == 0:
+                for t in range(PHASES):
+                    first[t, pl.ds(GUARD - 1, 1), :] = first[t, pl.ds(GUARD, 1), :]
     for copy in copies:
         copy.wait()
 
@@ -477,7 +521,6 @@
 
     assert rows % LANES == 0 and rows + HALO <= PHASES * (LANES - MARGIN) and PRE + POST <= HALO
     tall = pltpu.VMEM((PHASES, cells + 2 * GUARD, LANES), F32)
-    coefs = pltpu.VMEM((2, cells + 2 * GUARD, LANES), F32)
     flat = pltpu.VMEM((cells, PHASES * LANES), BF16)
     each = parcel_rows(rows)
 
@@ -486,26 +529,42 @@
         return in_vmem(lax.all_to_all(flat_parcels, AXES, 0, 0, tiled=True).reshape(devices * each, LANES))
 
     parcels_shape = pltpu.VMEM((devices * each, LANES), F32)
-    advanced, parcels = pl.pallas_call(
-        functools.partial(advance_kernel, devices=devices),
-        out_shape=(pltpu.VMEM((PHASES, cells, LANES), F32), parcels_shape),
-        in_specs=[smem, smem, hbm, vmem, vmem, hbm, hbm],
+    limits = pltpu.CompilerParams(vmem_limit_bytes=VMEM_LIMIT)
+    turned, coef = pl.pallas_call(
+        turn_kernel,
+        out_shape=(
+            pltpu.VMEM((PHASES, cells, LANES), F32),
+            pltpu.VMEM((2, cells + 2 * GUARD, LANES), F32),
+        ),
+        in_specs=[smem, hbm],
         out_specs=(vmem, vmem),
         scratch_shapes=[
             pltpu.VMEM((blocks, PHASES * LANES, LANES), F32),
+            pltpu.SemaphoreType.DMA((blocks,)),
+        ],
+        compiler_params=limits,
+        name="turn",
+    )(in_hbm(levels), in_hbm(density))
+
+    advanced, parcels = pl.pallas_call(
+        functools.partial(advance_kernel, devices=devices, rows=rows),
+        out_shape=(pltpu.VMEM((PHASES, cells, LANES), F32), parcels_shape),
+        in_specs=[smem, smem, vmem, vmem, vmem, vmem, hbm, hbm],
+        out_specs=(vmem, vmem),
+        scratch_shapes=[
             tall,
             tall,
-            coefs,
+            pltpu.VMEM((blocks, 2 * HALO, LANES), F32),
+            pltpu.VMEM((blocks, LANES, LANES), F32),
             flat,
             flat,
             pltpu.VMEM((MV, cells), BF16),
             pltpu.VMEM((MV, cells), BF16),
-            pltpu.SemaphoreType.DMA((blocks,)),
             pltpu.SemaphoreType.DMA((2,)),
         ],
-        compiler_params=pltpu.CompilerParams(vmem_limit_bytes=VMEM_LIMIT),
+        compiler_params=limits,
         name="advance",
-    )(in_hbm(levels), coeffs, in_hbm(density), above, below, in_hbm(bvt_high), in_hbm(bvt_low))
+    )(in_hbm(levels), coeffs, turned, coef, above, below, in_hbm(bvt_high), in_hbm(bvt_low))
 
     parcels = pl.pallas_call(
         functools.partial(combine_kernel, groups=groups, slabs=slabs, modes=modes),
@@ -513,28 +572,27 @@
         in_specs=[vmem] * 6,
         out_specs=vmem,
         scratch_shapes=[pltpu.VMEM((8 * groups * (slabs + 1), 2 * rows), F32)],
-        compiler_params=pltpu.CompilerParams(vmem_limit_bytes=VMEM_LIMIT),
+        compiler_params=limits,
         name="combine",
     )(exchange(parcels), *map(in_vmem, tables_x))
 
     result = pl.pallas_call(
         functools.partial(correct_kernel, devices=devices),
         out_shape=jax.ShapeDtypeStruct((rows, cells), F32),
-        in_specs=[smem, vmem, vmem, vmem, vmem],
+        in_specs=[smem] + [vmem] * 5,
         out_specs=hbm,
         scratch_shapes=[
             tall,
             tall,
-            coefs,
             pltpu.VMEM((2, PHASES, LANES, LANES), F32),
             pltpu.VMEM((blocks, rows, LANES), F32),
             pltpu.VMEM((MV, rows), F32),
             pltpu.VMEM((MV, LANES), F32),
             pltpu.SemaphoreType.DMA((1,)),
         ],
-        compiler_params=pltpu.CompilerParams(vmem_limit_bytes=VMEM_LIMIT),
+        compiler_params=limits,
         name="correct",
-    )(in_hbm(levels), advanced, exchange(parcels), in_vmem(bv_high), in_vmem(bv_low))
+    )(in_hbm(levels), advanced, coef, exchange(parcels), in_vmem(bv_high), in_vmem(bv_low))
     return result[None]
 
 

time: 66.1 us -> 63.9 us (0.967)
  blocking collectives: 31.4 us -> 35.5 us
  waiting for transfers between devices: 5.54 us -> 1.62 us
  Pallas kernels: 22.6 us -> 19.6 us
    all_to_all x2, blocking collectives: 31.4 us -> 35.5 us  [exchange(): lax.all_to_all(flat_parcels, AXES, 0, 0, tiled=True)]
    ppermute x1, waiting for transfers between devices: 3.67 us -> 1.62 us  [body(): above = in_vmem(lax.ppermute(density[rows - HALO:], 'dom', ring))]
    pallas_call x1 -> x2, Pallas kernels: 14.1 us -> 12.2 us  [the longest x1 8.3 us: body(): pl.pallas_call(functools.partial(advance_kernel, devices=devices, rows=ro...]
    ppermute x1, waiting for transfers between devices: 1.87 us -> 0.01 us  [body(): lax.ppermute(density[:HALO], 'dom', [(b, a) for a, b in ring])]
    pallas_call x1, Pallas kernels: 6.54 us -> 5.39 us  [body(): pl.pallas_call(functools.partial(correct_kernel, devices=devices), out_sh...]
  transfers between devices with their start and end apart: 2 -> 2, of which waited for: 2 -> 1; matrix products, arithmetic and copies ran while one was open for 0% -> 0% of each run, Pallas kernels for 0% -> 6%
where the time goes in v4:
time: 63.9 us; the launch traced here: 63.2 us
  blocking collectives  35.5 us (56%)
  Pallas kernels  19.6 us (31%)
  starting transfers between devices  4.57 us (7%)
  waiting for transfers between devices  1.62 us (3%)
  local copies, waits for them, and re-layouts  1.02 us (2%)
  between operations  0.9 us (1%)
    all_to_all x2, blocking collectives, exchange(): lax.all_to_all(flat_parcels, AXES, 0, 0, tiled=True)  35.5 us
    pallas_call x1, Pallas kernels, body(): pl.pallas_call(functools.partial(advance_kernel, devices=devices, rows=ro...  8.3 us
    pallas_call x1, Pallas kernels, body(): pl.pallas_call(functools.partial(correct_kernel, devices=devices), out_sh...  5.39 us
    ppermute x1, starting transfers between devices, body(): lax.ppermute(density[:HALO], 'dom', [(b, a) for a, b in ring])  4.57 us
    pallas_call x1, Pallas kernels, body(): pl.pallas_call(turn_kernel, out_shape=(pltpu.VMEM((PHASES, cells, LANES),...  3.9 us
    pallas_call x1, Pallas kernels, body(): pl.pallas_call(functools.partial(combine_kernel, groups=groups, slabs=sla...  1.98 us
    ppermute x1, waiting for transfers between devices, body(): above = in_vmem(lax.ppermute(density[rows - HALO:], 'dom', ring))  1.62 us
  transfers between devices with their start and end apart: 2, of which 1 were waited for; matrix products, arithmetic and copies ran while one was open for 0% of the time, Pallas kernels for 6%

profile of v4, /device:TPU:0, one launch (start us, length us, event | category | flops | bytes accessed | tf_op | source)
XLA Modules:
  0.0 63.2 jit_solution(331767716382190794)
XLA Ops:
  0.0 1.0 %slice_bitcast_fusion = (f32[16,2048]{1,0:T(8,128)S(1)}, f32[16,2048]{1,0:T(8,128)S(1)}) fusion(f32[1,384,2048]{2,1,0:T(8,128)} %param.12), kind=kLoop, calls=%fused_computation | loop fusion | bytes 524288 | tf_op jit(solution)/shard_map/slice | solution.py:520
  1.0 4.6 %collective-permute-start.1 = (f32[16,2048]{1,0:T(8,128)S(1)}, f32[16,2048]{1,0:T(8,128)S(1)}, u32[]{:S(2)}, u32[]{:S(2)}) collective-permute-start(f32[16,2048]{1,0:T(8,128)S(1)} %get-tuple-element.13), channel_id=1, source_target_pairs={{1,0},{2,1},{3,2},{4,3},{5,4},{6,5},{7,6},{0,7},{9,8},{10,9},{11,1... | collective-permute-start | bytes 393224 | tf_op jit(solution)/shard_map/ppermute | solution.py:520
  5.6 0.0 collective-permute-start
  6.2 3.9 %turn.1 = (f32[4,2048,128]{2,1,0:T(8,128)S(1)}, f32[2,2064,128]{2,1,0:T(8,128)S(1)}) custom-call(s32[1,2]{1,0:T(1,128)} %levels.5, f32[384,2048]{1,0:T(8,128)} %bitcast.14), custom_call_target="tpu_custom_call" | custom-call | tf_op jit(solution)/shard_map/turn/pallas_call | solution.py:533
  10.1 0.0 collective-permute-done.1.below
  10.1 1.6 %collective-permute-done.above = f32[16,2048]{1,0:T(8,128)S(1)} collective-permute-done((f32[16,2048]{1,0:T(8,128)S(1)}, f32[16,2048]{1,0:T(8,128)S(1)}, u32[]{:S(2)}, u32[]{:S(2)}) %collective-permute-start) | collective-permute-done | bytes 131104 | tf_op jit(solution)/shard_map/ppermute | solution.py:519
  11.8 0.0 copy-start.2
  11.8 0.0 copy-start.3
  11.8 0.0 copy-start.4
  11.8 0.0 copy-start.5
  11.8 0.0 copy-start.6
  11.8 8.3 %advance.1 = (f32[4,2048,128]{2,1,0:T(8,128)S(1)}, f32[800,128]{1,0:T(8,128)S(1)}) custom-call(s32[1,2]{1,0:T(1,128)} %levels.5, s32[1]{0:T(128)S(6)} %copy.15.coeffs, f32[4,2048,128]{2,1,0:T(8,128)S(1)} %get-tuple-element.9.turned, f32[2,2064,128]{2,1,0:T(8,128)S(1)} %get-tuple-element.10.coef, f32[16,2048]{1,0:T(8,128)S(1)} %collective-permute-done.above, ...), custom_call_target="tpu_custom_call" | custom-call | tf_op jit(solution)/shard_map/advance/pallas_call | solution.py:549
  20.1 0.0 copy-start
  20.1 0.0 copy-start.1
  20.1 19.6 %all_to_all.10 = f32[32,1,3200]{2,1,0:T(1,128)S(1)} all-to-all(f32[32,1,3200]{2,1,0:T(1,128)S(1)} %bitcast.13), channel_id=1, replica_groups=mesh['comp'=4,'dom'=8] {'comp','dom'}, dimensions={0} | all-to-all | bytes 819200 | tf_op jit(solution)/shard_map/all_to_all | solution.py:529
  39.7 0.0 copy-done.2
  39.7 0.0 copy-done.3
  39.7 0.0 copy-done.4
  39.8 0.0 copy-done.5
  39.8 0.0 copy-done.6
  39.8 2.0 %combine.1 = f32[800,128]{1,0:T(8,128)S(1)} custom-call(f32[800,128]{1,0:T(8,128)S(1)} %bitcast.10, f32[2,9,1,384]{3,2,1,0:T(1,128)S(1)} %copy-done.6, bf16[768,256]{1,0:T(8,128)(2,1)S(1)} %copy-done.5, bf16[768,256]{1,0:T(8,128)(2,1)S(1)} %copy-done.4, bf16[256,768]{1,0:T(8,128)(2,1)S(1)} %copy-done.3, bf16[256,768]{1,0:T(8,128)(2,1)S(1)} %copy-done.2), custom_call_target="tpu_custom_call" | custom-call | tf_op jit(solution)/shard_map/combine/pallas_call | solution.py:569
  41.8 15.9 %all_to_all.11 = f32[32,1,3200]{2,1,0:T(1,128)S(1)} all-to-all(f32[32,1,3200]{2,1,0:T(1,128)S(1)} %bitcast.11), channel_id=1, replica_groups=mesh['comp'=4,'dom'=8] {'comp','dom'}, dimensions={0} | all-to-all | bytes 819200 | tf_op jit(solution)/shard_map/all_to_all | solution.py:529
  57.6 0.0 copy-done
  57.6 0.0 copy-done.1
  57.6 5.4 %correct.1 = f32[384,2048]{1,0:T(8,128)} custom-call(s32[1,2]{1,0:T(1,128)} %levels.5, f32[4,2048,128]{2,1,0:T(8,128)S(1)} %get-tuple-element.11.advanced, f32[2,2064,128]{2,1,0:T(8,128)S(1)} %get-tuple-element.10.coef, f32[800,128]{1,0:T(8,128)S(1)} %bitcast.12, bf16[2048,256]{1,0:T(8,128)(2,1)S(1)} %copy-done.1, bf16[2048,256]{1,0:T(8,128)(2,1)S(1)} %copy-done), custom_call_target="tpu_custom_call" | custom-call | tf_op jit(solution)/shard_map/correct/pallas_call | solution.py:579
Async XLA Ops:
  1.0 9.1 %collective-permute-start.1 = (f32[16,2048]{1,0:T(8,128)S(1)}, f32[16,2048]{1,0:T(8,128)S(1)}, u32[]{:S(2)}, u32[]{:S(2)}) collective-permute-start(f32[16,2048]{1,0:T(8,128)S(1)} %get-tuple-element.13), channel_id=1, source_target_pairs={{1,0},{2,1},{3,2},{4,3},{5,4},{6,5},{7,6},{0,7},{9,8},{10,9},{11,1... | collective-permute-start | bytes 393224 | tf_op jit(solution)/shard_map/ppermute | solution.py:520
  5.6 6.2 %collective-permute-start = (f32[16,2048]{1,0:T(8,128)S(1)}, f32[16,2048]{1,0:T(8,128)S(1)}, u32[]{:S(2)}, u32[]{:S(2)}) collective-permute-start(f32[16,2048]{1,0:T(8,128)S(1)} %get-tuple-element.14), channel_id=1, source_target_pairs={{0,1},{1,2},{2,3},{3,4},{4,5},{5,6},{6,7},{7,0},{8,9},{9,10},{10,1... | collective-permute-start | bytes 393224 | tf_op jit(solution)/shard_map/ppermute | solution.py:519
  11.8 28.0 %copy-start.2 = (bf16[256,768]{1,0:T(8,128)(2,1)S(1)}, bf16[256,768]{1,0:T(8,128)(2,1)}, u32[]{:S(2)}) copy-start(bf16[256,768]{1,0:T(8,128)(2,1)} %constant.24.clone.back_low) | copy-start | bytes 1179652
  11.8 28.0 %copy-start.3 = (bf16[256,768]{1,0:T(8,128)(2,1)S(1)}, bf16[256,768]{1,0:T(8,128)(2,1)}, u32[]{:S(2)}) copy-start(bf16[256,768]{1,0:T(8,128)(2,1)} %constant.23.clone.back_high) | copy-start | bytes 1179652
  11.8 28.0 %copy-start.4 = (bf16[768,256]{1,0:T(8,128)(2,1)S(1)}, bf16[768,256]{1,0:T(8,128)(2,1)}, u32[]{:S(2)}) copy-start(bf16[768,256]{1,0:T(8,128)(2,1)} %constant.22.clone.ahead_low) | copy-start | bytes 1179652
  11.8 28.0 %copy-start.5 = (bf16[768,256]{1,0:T(8,128)(2,1)S(1)}, bf16[768,256]{1,0:T(8,128)(2,1)}, u32[]{:S(2)}) copy-start(bf16[768,256]{1,0:T(8,128)(2,1)} %constant.21.clone.ahead_high) | copy-start | bytes 1179652
  11.8 28.0 %copy-start.6 = (f32[2,9,1,384]{3,2,1,0:T(1,128)S(1)}, f32[2,9,1,384]{3,2,1,0:T(1,128)}, u32[]{:S(2)}) copy-start(f32[2,9,1,384]{3,2,1,0:T(1,128)} %constant.20.clone.twiddle) | copy-start | bytes 82948
  20.1 37.6 %copy-start = (bf16[2048,256]{1,0:T(8,128)(2,1)S(1)}, bf16[2048,256]{1,0:T(8,128)(2,1)}, u32[]{:S(2)}) copy-start(bf16[2048,256]{1,0:T(8,128)(2,1)} %constant.26.clone.bv_low) | copy-start | bytes 3145732
  20.1 37.6 %copy-start.1 = (bf16[2048,256]{1,0:T(8,128)(2,1)S(1)}, bf16[2048,256]{1,0:T(8,128)(2,1)}, u32[]{:S(2)}) copy-start(bf16[2048,256]{1,0:T(8,128)(2,1)} %constant.25.clone.bv_high) | copy-start | bytes 3145732

commit v5 on v4

--- a/solution.py
+++ b/solution.py
@@ -14,7 +14,7 @@
 PRE = 8
 POST = 2
 LANES = 128
-HALO = 16
+HALO = 12
 PHASES = 4
 MARGIN = 8
 GUARD = 8
@@ -90,7 +90,7 @@
 
 
 def inner_step(src, dst, coef, cells):
-    unroll = 32
+    unroll = 64
     for leftward in (True, False):
         start = GUARD if leftward else GUARD + cells // 2
 
@@ -184,8 +184,9 @@
     def insert(target):
         for c in range(planes):
             lanes = pl.ds(c * LANES, LANES)
-            halos[c, pl.ds(0, HALO), :] = above[:, lanes]
-            halos[c, pl.ds(HALO, HALO), :] = below[:, lanes]
+            for a in range(run):
+                halos[c, pl.ds(PHASES * a, PHASES), :] = above[a, :, lanes]
+                halos[c, pl.ds(HALO + PHASES * a, PHASES), :] = below[a, :, lanes]
             for t in range(PHASES):
                 for low_lane, row in sides:
                     at = (low_lane + shift * t) % LANES
@@ -516,8 +517,10 @@
     smem = pl.BlockSpec(memory_space=pltpu.SMEM)
     hbm = pl.BlockSpec(memory_space=pl.ANY)
     ring = [(i, (i + 1) % slabs) for i in range(slabs)]
-    above = in_vmem(lax.ppermute(density[rows - HALO :], "dom", ring))
-    below = in_vmem(lax.ppermute(density[:HALO], "dom", [(b, a) for a, b in ring]))
+    tail = jnp.stack([density[at : at + PHASES] for at in range(rows - HALO, rows, PHASES)])
+    head = jnp.stack([density[at : at + PHASES] for at in range(0, HALO, PHASES)])
+    above = in_vmem(lax.ppermute(tail, "dom", ring))
+    below = in_vmem(lax.ppermute(head, "dom", [(b, a) for a, b in ring]))
 
     assert rows % LANES == 0 and rows + HALO <= PHASES * (LANES - MARGIN) and PRE + POST <= HALO
     tall = pltpu.VMEM((PHASES, cells + 2 * GUARD, LANES), F32)

time: 63.9 us -> 62.2 us (0.973)
  Pallas kernels: 19.6 us -> 21.3 us
  waiting for transfers between devices: 1.62 us -> 0.01 us
  blocking collectives: 35.5 us -> 33.9 us
    pallas_call x1, Pallas kernels: 8.3 us -> 10 us  [body(): pl.pallas_call(functools.partial(advance_kernel, devices=devices, rows=ro...]
    ppermute x2, waiting for transfers between devices: 1.62 us -> 0.01 us  [the longest x1 0.01 us: body(): below = in_vmem(lax.ppermute(head, 'dom', [(b, a) for a, b in ring]))]
    all_to_all x2, blocking collectives: 35.5 us -> 33.9 us  [exchange(): lax.all_to_all(flat_parcels, AXES, 0, 0, tiled=True)]
  transfers between devices with their start and end apart: 2 -> 2, of which waited for: 1 -> 0; matrix products, arithmetic and copies ran while one was open for 0% -> 0% of each run, Pallas kernels for 6% -> 6%
where the time goes in v5:
time: 62.2 us; the launch traced here: 61.9 us
  blocking collectives  33.9 us (55%)
  Pallas kernels  21.3 us (34%)
  starting transfers between devices  4.64 us (7%)
  local copies, waits for them, and re-layouts  1.08 us (2%)
  between operations  0.94 us (2%)
    all_to_all x2, blocking collectives, exchange(): lax.all_to_all(flat_parcels, AXES, 0, 0, tiled=True)  33.9 us
    pallas_call x1, Pallas kernels, body(): pl.pallas_call(functools.partial(advance_kernel, devices=devices, rows=ro...  10 us
    pallas_call x1, Pallas kernels, body(): pl.pallas_call(functools.partial(correct_kernel, devices=devices), out_sh...  5.38 us
    ppermute x1, starting transfers between devices, body(): below = in_vmem(lax.ppermute(head, 'dom', [(b, a) for a, b in ring]))  4.1 us
    pallas_call x1, Pallas kernels, body(): pl.pallas_call(turn_kernel, out_shape=(pltpu.VMEM((PHASES, cells, LANES),...  3.9 us
    pallas_call x1, Pallas kernels, body(): pl.pallas_call(functools.partial(combine_kernel, groups=groups, slabs=sla...  1.98 us
  transfers between devices with their start and end apart: 2, of which 0 were waited for; matrix products, arithmetic and copies ran while one was open for 0% of the time, Pallas kernels for 6%

profile of v5, /device:TPU:0, one launch (start us, length us, event | category | flops | bytes accessed | tf_op | source)
XLA Modules:
  0.0 61.9 jit_solution(5335002324590505872)
XLA Ops:
  0.0 1.0 %fusion = (f32[1,4,2048]{2,1,0:T(4,128)S(1)}, f32[1,4,2048]{2,1,0:T(4,128)S(1)}, f32[1,4,2048]{2,1,0:T(4,128)S(1)}, f32[1,4,2048]{2,1,0:T(4,128)S(1)}, f32[1,4,2048]{2,1,0:T(4,128)S(1)}, /*index=5*/f32[1,4,2048]{2,1,0:T(4,128)S(1)}) fusion(f32[1,384,2048]{2,1,0:T(8,128)} %param.12), kind=kLoop, calls=%fused_computation.2 | loop fusion | bytes 393216 | tf_op jit(solution)/shard_map/slice | solution.py:521
  1.1 0.5 collective-permute-start
  1.6 4.1 %collective-permute-start.1 = (f32[3,4,2048]{2,1,0:T(4,128)S(1)}, f32[3,4,2048]{2,1,0:T(4,128)S(1)}, u32[]{:S(2)}, u32[]{:S(2)}) collective-permute-start(f32[3,4,2048]{2,1,0:T(4,128)S(1)} %pad_maximum_fusion.1), channel_id=1, source_target_pairs={{1,0},{2,1},{3,2},{4,3},{5,4},{6,5},{7,6},{0,7},{9,8},{10,9},{11,1... | collective-permute-start | bytes 294920 | tf_op jit(solution)/shard_map/ppermute | solution.py:523
  6.4 3.9 %turn.1 = (f32[4,2048,128]{2,1,0:T(8,128)S(1)}, f32[2,2064,128]{2,1,0:T(8,128)S(1)}) custom-call(s32[1,2]{1,0:T(1,128)} %levels.5, f32[384,2048]{1,0:T(8,128)} %bitcast.10), custom_call_target="tpu_custom_call" | custom-call | tf_op jit(solution)/shard_map/turn/pallas_call | solution.py:536
  10.3 0.0 collective-permute-done.above
  10.3 0.0 collective-permute-done.1.below
  10.3 0.0 copy-start.2
  10.3 0.0 copy-start.3
  10.3 0.0 copy-start.4
  10.4 0.0 copy-start.5
  10.4 0.0 copy-start.6
  10.4 10.0 %advance.1 = (f32[4,2048,128]{2,1,0:T(8,128)S(1)}, f32[800,128]{1,0:T(8,128)S(1)}) custom-call(s32[1,2]{1,0:T(1,128)} %levels.5, s32[1]{0:T(128)S(6)} %copy.15.coeffs, f32[4,2048,128]{2,1,0:T(8,128)S(1)} %get-tuple-element.9.turned, f32[2,2064,128]{2,1,0:T(8,128)S(1)} %get-tuple-element.10.coef, f32[3,4,2048]{2,1,0:T(4,128)S(1)} %collective-permute-done.above, ...), custom_call_target="tpu_custom_call" | custom-call | tf_op jit(solution)/shard_map/advance/pallas_call | solution.py:552
  20.4 0.0 copy-start
  20.4 0.0 copy-start.1
  20.4 18.1 %all_to_all.10 = f32[32,1,3200]{2,1,0:T(1,128)S(1)} all-to-all(f32[32,1,3200]{2,1,0:T(1,128)S(1)} %bitcast.9), channel_id=1, replica_groups=mesh['comp'=4,'dom'=8] {'comp','dom'}, dimensions={0} | all-to-all | bytes 819200 | tf_op jit(solution)/shard_map/all_to_all | solution.py:532
  38.5 0.0 copy-done.2
  38.5 0.0 copy-done.3
  38.5 0.0 copy-done.4
  38.5 0.0 copy-done.5
  38.5 0.0 copy-done.6
  38.5 2.0 %combine.1 = f32[800,128]{1,0:T(8,128)S(1)} custom-call(f32[800,128]{1,0:T(8,128)S(1)} %bitcast.6, f32[2,9,1,384]{3,2,1,0:T(1,128)S(1)} %copy-done.6, bf16[768,256]{1,0:T(8,128)(2,1)S(1)} %copy-done.5, bf16[768,256]{1,0:T(8,128)(2,1)S(1)} %copy-done.4, bf16[256,768]{1,0:T(8,128)(2,1)S(1)} %copy-done.3, bf16[256,768]{1,0:T(8,128)(2,1)S(1)} %copy-done.2), custom_call_target="tpu_custom_call" | custom-call | tf_op jit(solution)/shard_map/combine/pallas_call | solution.py:572
  40.5 15.9 %all_to_all.11 = f32[32,1,3200]{2,1,0:T(1,128)S(1)} all-to-all(f32[32,1,3200]{2,1,0:T(1,128)S(1)} %bitcast.7), channel_id=1, replica_groups=mesh['comp'=4,'dom'=8] {'comp','dom'}, dimensions={0} | all-to-all | bytes 819200 | tf_op jit(solution)/shard_map/all_to_all | solution.py:532
  56.4 0.0 copy-done
  56.4 0.0 copy-done.1
  56.4 5.4 %correct.1 = f32[384,2048]{1,0:T(8,128)} custom-call(s32[1,2]{1,0:T(1,128)} %levels.5, f32[4,2048,128]{2,1,0:T(8,128)S(1)} %get-tuple-element.11.advanced, f32[2,2064,128]{2,1,0:T(8,128)S(1)} %get-tuple-element.10.coef, f32[800,128]{1,0:T(8,128)S(1)} %bitcast.8, bf16[2048,256]{1,0:T(8,128)(2,1)S(1)} %copy-done.1, bf16[2048,256]{1,0:T(8,128)(2,1)S(1)} %copy-done), custom_call_target="tpu_custom_call" | custom-call | tf_op jit(solution)/shard_map/correct/pallas_call | solution.py:582
  (2 shorter events, 0.0 us)
Async XLA Ops:
  1.1 9.2 %collective-permute-start = (f32[3,4,2048]{2,1,0:T(4,128)S(1)}, f32[3,4,2048]{2,1,0:T(4,128)S(1)}, u32[]{:S(2)}, u32[]{:S(2)}) collective-permute-start(f32[3,4,2048]{2,1,0:T(4,128)S(1)} %pad_maximum_fusion), channel_id=1, source_target_pairs={{0,1},{1,2},{2,3},{3,4},{4,5},{5,6},{6,7},{7,0},{8,9},{9,10},{10,1... | collective-permute-start | bytes 294920 | tf_op jit(solution)/shard_map/ppermute | solution.py:522
  1.6 8.7 %collective-permute-start.1 = (f32[3,4,2048]{2,1,0:T(4,128)S(1)}, f32[3,4,2048]{2,1,0:T(4,128)S(1)}, u32[]{:S(2)}, u32[]{:S(2)}) collective-permute-start(f32[3,4,2048]{2,1,0:T(4,128)S(1)} %pad_maximum_fusion.1), channel_id=1, source_target_pairs={{1,0},{2,1},{3,2},{4,3},{5,4},{6,5},{7,6},{0,7},{9,8},{10,9},{11,1... | collective-permute-start | bytes 294920 | tf_op jit(solution)/shard_map/ppermute | solution.py:523
  10.3 28.2 %copy-start.2 = (bf16[256,768]{1,0:T(8,128)(2,1)S(1)}, bf16[256,768]{1,0:T(8,128)(2,1)}, u32[]{:S(2)}) copy-start(bf16[256,768]{1,0:T(8,128)(2,1)} %constant.24.clone.back_low) | copy-start | bytes 1179652
  10.3 28.1 %copy-start.3 = (bf16[256,768]{1,0:T(8,128)(2,1)S(1)}, bf16[256,768]{1,0:T(8,128)(2,1)}, u32[]{:S(2)}) copy-start(bf16[256,768]{1,0:T(8,128)(2,1)} %constant.23.clone.back_high) | copy-start | bytes 1179652
  10.3 28.1 %copy-start.4 = (bf16[768,256]{1,0:T(8,128)(2,1)S(1)}, bf16[768,256]{1,0:T(8,128)(2,1)}, u32[]{:S(2)}) copy-start(bf16[768,256]{1,0:T(8,128)(2,1)} %constant.22.clone.ahead_low) | copy-start | bytes 1179652
  10.4 28.1 %copy-start.5 = (bf16[768,256]{1,0:T(8,128)(2,1)S(1)}, bf16[768,256]{1,0:T(8,128)(2,1)}, u32[]{:S(2)}) copy-start(bf16[768,256]{1,0:T(8,128)(2,1)} %constant.21.clone.ahead_high) | copy-start | bytes 1179652
  10.4 28.1 %copy-start.6 = (f32[2,9,1,384]{3,2,1,0:T(1,128)S(1)}, f32[2,9,1,384]{3,2,1,0:T(1,128)}, u32[]{:S(2)}) copy-start(f32[2,9,1,384]{3,2,1,0:T(1,128)} %constant.20.clone.twiddle) | copy-start | bytes 82948
  20.4 36.0 %copy-start = (bf16[2048,256]{1,0:T(8,128)(2,1)S(1)}, bf16[2048,256]{1,0:T(8,128)(2,1)}, u32[]{:S(2)}) copy-start(bf16[2048,256]{1,0:T(8,128)(2,1)} %constant.26.clone.bv_low) | copy-start | bytes 3145732
  20.4 36.0 %copy-start.1 = (bf16[2048,256]{1,0:T(8,128)(2,1)S(1)}, bf16[2048,256]{1,0:T(8,128)(2,1)}, u32[]{:S(2)}) copy-start(bf16[2048,256]{1,0:T(8,128)(2,1)} %constant.25.clone.bv_high) | copy-start | bytes 3145732

commit v6 on v5

--- a/solution.py
+++ b/solution.py
@@ -43,6 +43,14 @@
 
 def dot(a, b, dims=((1,), (0,))):
     return lax.dot_general(a, b, (dims, ((), ())), preferred_element_type=F32)
+
+
+def split_dot(high, low, right_high, right_low):
+    half = high.shape[0] // 2
+    parts = []
+    for rows in (slice(0, half), slice(half, None)):
+        parts.append(dot(high[rows], right_high) + dot(low[rows], right_high) + dot(high[rows], right_low))
+    return jnp.concatenate(parts, axis=0)
 
 
 def rates(levels_ref):
@@ -346,7 +354,7 @@
                 waves[where, lanes] = turned[0]
                 waves[where, pl.ds(slab_rows + j * LANES, LANES)] = turned[1]
     high, low = split(waves[...])
-    projected = dot(high, ahead_high[...]) + dot(low, ahead_high[...]) + dot(high, ahead_low[...])
+    projected = split_dot(high, low, ahead_high[...], ahead_low[...])
     width = projected.shape[1]
     own = lax.axis_index(AXES[0]) * slabs + lax.axis_index(AXES[1])
     row_mode = (own * modes + lax.broadcasted_iota(jnp.int32, (8, width), 0)).astype(F32)
@@ -376,7 +384,7 @@
             combined = part if combined is None else combined + part
         changes += [combined - surplus for surplus in surpluses]
     high, low = split(jnp.concatenate(changes, axis=0))
-    waves[...] = dot(high, back_high[...]) + dot(low, back_high[...]) + dot(high, back_low[...])
+    waves[...] = split_dot(high, low, back_high[...], back_low[...])
     for g in range(groups):
         for j in range(parts):
             lanes = pl.ds(j * LANES, LANES)

time: 62.2 us -> 61.9 us (level); the launches traced: 61.9 us -> 60.7 us
  Pallas kernels: 21.3 us -> 20 us
    pallas_call x1, Pallas kernels: 10 us -> 9.12 us  [body(): pl.pallas_call(functools.partial(advance_kernel, devices=devices, rows=ro...]
where the time goes in v6:
time: 61.9 us; the launch traced here: 60.7 us
  blocking collectives  34 us (55%)
  Pallas kernels  20 us (32%)
  starting transfers between devices  4.64 us (7%)
  local copies, waits for them, and re-layouts  1.08 us (2%)
  between operations  0.94 us (2%)
    all_to_all x2, blocking collectives, exchange(): lax.all_to_all(flat_parcels, AXES, 0, 0, tiled=True)  34 us
    pallas_call x1, Pallas kernels, body(): pl.pallas_call(functools.partial(advance_kernel, devices=devices, rows=ro...  9.12 us
    pallas_call x1, Pallas kernels, body(): pl.pallas_call(functools.partial(correct_kernel, devices=devices), out_sh...  5.39 us
    ppermute x1, starting transfers between devices, body(): below = in_vmem(lax.ppermute(head, 'dom', [(b, a) for a, b in ring]))  4.1 us
    pallas_call x1, Pallas kernels, body(): pl.pallas_call(turn_kernel, out_shape=(pltpu.VMEM((PHASES, cells, LANES),...  3.9 us
    pallas_call x1, Pallas kernels, body(): pl.pallas_call(functools.partial(combine_kernel, groups=groups, slabs=sla...  1.63 us
  transfers between devices with their start and end apart: 2, of which 0 were waited for; matrix products, arithmetic and copies ran while one was open for 0% of the time, Pallas kernels for 6%

profile of v6, /device:TPU:0, one launch (start us, length us, event | category | flops | bytes accessed | tf_op | source)
XLA Modules:
  0.0 60.7 jit_solution(9389452369684326056)
XLA Ops:
  0.0 1.0 %fusion = (f32[1,4,2048]{2,1,0:T(4,128)S(1)}, f32[1,4,2048]{2,1,0:T(4,128)S(1)}, f32[1,4,2048]{2,1,0:T(4,128)S(1)}, f32[1,4,2048]{2,1,0:T(4,128)S(1)}, f32[1,4,2048]{2,1,0:T(4,128)S(1)}, /*index=5*/f32[1,4,2048]{2,1,0:T(4,128)S(1)}) fusion(f32[1,384,2048]{2,1,0:T(8,128)} %param.12), kind=kLoop, calls=%fused_computation.2 | loop fusion | bytes 393216 | tf_op jit(solution)/shard_map/slice | solution.py:529
  1.1 0.5 collective-permute-start
  1.6 4.1 %collective-permute-start.1 = (f32[3,4,2048]{2,1,0:T(4,128)S(1)}, f32[3,4,2048]{2,1,0:T(4,128)S(1)}, u32[]{:S(2)}, u32[]{:S(2)}) collective-permute-start(f32[3,4,2048]{2,1,0:T(4,128)S(1)} %pad_maximum_fusion.1), channel_id=1, source_target_pairs={{1,0},{2,1},{3,2},{4,3},{5,4},{6,5},{7,6},{0,7},{9,8},{10,9},{11,1... | collective-permute-start | bytes 294920 | tf_op jit(solution)/shard_map/ppermute | solution.py:531
  6.4 3.9 %turn.1 = (f32[4,2048,128]{2,1,0:T(8,128)S(1)}, f32[2,2064,128]{2,1,0:T(8,128)S(1)}) custom-call(s32[1,2]{1,0:T(1,128)} %levels.5, f32[384,2048]{1,0:T(8,128)} %bitcast.10), custom_call_target="tpu_custom_call" | custom-call | tf_op jit(solution)/shard_map/turn/pallas_call | solution.py:544
  10.3 0.0 collective-permute-done.above
  10.3 0.0 collective-permute-done.1.below
  10.3 0.0 copy-start.2
  10.3 0.0 copy-start.3
  10.3 0.0 copy-start.4
  10.4 0.0 copy-start.5
  10.4 0.0 copy-start.6
  10.4 9.1 %advance.1 = (f32[4,2048,128]{2,1,0:T(8,128)S(1)}, f32[800,128]{1,0:T(8,128)S(1)}) custom-call(s32[1,2]{1,0:T(1,128)} %levels.5, s32[1]{0:T(128)S(6)} %copy.15.coeffs, f32[4,2048,128]{2,1,0:T(8,128)S(1)} %get-tuple-element.9.turned, f32[2,2064,128]{2,1,0:T(8,128)S(1)} %get-tuple-element.10.coef, f32[3,4,2048]{2,1,0:T(4,128)S(1)} %collective-permute-done.above, ...), custom_call_target="tpu_custom_call" | custom-call | tf_op jit(solution)/shard_map/advance/pallas_call | solution.py:560
  19.5 0.0 copy-start
  19.5 0.0 copy-start.1
  19.5 18.1 %all_to_all.10 = f32[32,1,3200]{2,1,0:T(1,128)S(1)} all-to-all(f32[32,1,3200]{2,1,0:T(1,128)S(1)} %bitcast.9), channel_id=1, replica_groups=mesh['comp'=4,'dom'=8] {'comp','dom'}, dimensions={0} | all-to-all | bytes 819200 | tf_op jit(solution)/shard_map/all_to_all | solution.py:540
  37.6 0.0 copy-done.2
  37.6 0.0 copy-done.3
  37.6 0.0 copy-done.4
  37.6 0.0 copy-done.5
  37.6 0.0 copy-done.6
  37.6 1.6 %combine.1 = f32[800,128]{1,0:T(8,128)S(1)} custom-call(f32[800,128]{1,0:T(8,128)S(1)} %bitcast.6, f32[2,9,1,384]{3,2,1,0:T(1,128)S(1)} %copy-done.6, bf16[768,256]{1,0:T(8,128)(2,1)S(1)} %copy-done.5, bf16[768,256]{1,0:T(8,128)(2,1)S(1)} %copy-done.4, bf16[256,768]{1,0:T(8,128)(2,1)S(1)} %copy-done.3, bf16[256,768]{1,0:T(8,128)(2,1)S(1)} %copy-done.2), custom_call_target="tpu_custom_call" | custom-call | tf_op jit(solution)/shard_map/combine/pallas_call | solution.py:580
  39.3 15.9 %all_to_all.11 = f32[32,1,3200]{2,1,0:T(1,128)S(1)} all-to-all(f32[32,1,3200]{2,1,0:T(1,128)S(1)} %bitcast.7), channel_id=1, replica_groups=mesh['comp'=4,'dom'=8] {'comp','dom'}, dimensions={0} | all-to-all | bytes 819200 | tf_op jit(solution)/shard_map/all_to_all | solution.py:540
  55.2 0.0 copy-done
  55.2 0.0 copy-done.1
  55.2 5.4 %correct.1 = f32[384,2048]{1,0:T(8,128)} custom-call(s32[1,2]{1,0:T(1,128)} %levels.5, f32[4,2048,128]{2,1,0:T(8,128)S(1)} %get-tuple-element.11.advanced, f32[2,2064,128]{2,1,0:T(8,128)S(1)} %get-tuple-element.10.coef, f32[800,128]{1,0:T(8,128)S(1)} %bitcast.8, bf16[2048,256]{1,0:T(8,128)(2,1)S(1)} %copy-done.1, bf16[2048,256]{1,0:T(8,128)(2,1)S(1)} %copy-done), custom_call_target="tpu_custom_call" | custom-call | tf_op jit(solution)/shard_map/correct/pallas_call | solution.py:590
  (2 shorter events, 0.0 us)
Async XLA Ops:
  1.1 9.2 %collective-permute-start = (f32[3,4,2048]{2,1,0:T(4,128)S(1)}, f32[3,4,2048]{2,1,0:T(4,128)S(1)}, u32[]{:S(2)}, u32[]{:S(2)}) collective-permute-start(f32[3,4,2048]{2,1,0:T(4,128)S(1)} %pad_maximum_fusion), channel_id=1, source_target_pairs={{0,1},{1,2},{2,3},{3,4},{4,5},{5,6},{6,7},{7,0},{8,9},{9,10},{10,1... | collective-permute-start | bytes 294920 | tf_op jit(solution)/shard_map/ppermute | solution.py:530
  1.6 8.7 %collective-permute-start.1 = (f32[3,4,2048]{2,1,0:T(4,128)S(1)}, f32[3,4,2048]{2,1,0:T(4,128)S(1)}, u32[]{:S(2)}, u32[]{:S(2)}) collective-permute-start(f32[3,4,2048]{2,1,0:T(4,128)S(1)} %pad_maximum_fusion.1), channel_id=1, source_target_pairs={{1,0},{2,1},{3,2},{4,3},{5,4},{6,5},{7,6},{0,7},{9,8},{10,9},{11,1... | collective-permute-start | bytes 294920 | tf_op jit(solution)/shard_map/ppermute | solution.py:531
  10.3 27.3 %copy-start.2 = (bf16[256,768]{1,0:T(8,128)(2,1)S(1)}, bf16[256,768]{1,0:T(8,128)(2,1)}, u32[]{:S(2)}) copy-start(bf16[256,768]{1,0:T(8,128)(2,1)} %constant.24.clone.back_low) | copy-start | bytes 1179652
  10.3 27.3 %copy-start.3 = (bf16[256,768]{1,0:T(8,128)(2,1)S(1)}, bf16[256,768]{1,0:T(8,128)(2,1)}, u32[]{:S(2)}) copy-start(bf16[256,768]{1,0:T(8,128)(2,1)} %constant.23.clone.back_high) | copy-start | bytes 1179652
  10.3 27.3 %copy-start.4 = (bf16[768,256]{1,0:T(8,128)(2,1)S(1)}, bf16[768,256]{1,0:T(8,128)(2,1)}, u32[]{:S(2)}) copy-start(bf16[768,256]{1,0:T(8,128)(2,1)} %constant.22.clone.ahead_low) | copy-start | bytes 1179652
  10.4 27.3 %copy-start.5 = (bf16[768,256]{1,0:T(8,128)(2,1)S(1)}, bf16[768,256]{1,0:T(8,128)(2,1)}, u32[]{:S(2)}) copy-start(bf16[768,256]{1,0:T(8,128)(2,1)} %constant.21.clone.ahead_high) | copy-start | bytes 1179652
  10.4 27.3 %copy-start.6 = (f32[2,9,1,384]{3,2,1,0:T(1,128)S(1)}, f32[2,9,1,384]{3,2,1,0:T(1,128)}, u32[]{:S(2)}) copy-start(f32[2,9,1,384]{3,2,1,0:T(1,128)} %constant.20.clone.twiddle) | copy-start | bytes 82948
  19.5 35.6 %copy-start = (bf16[2048,256]{1,0:T(8,128)(2,1)S(1)}, bf16[2048,256]{1,0:T(8,128)(2,1)}, u32[]{:S(2)}) copy-start(bf16[2048,256]{1,0:T(8,128)(2,1)} %constant.26.clone.bv_low) | copy-start | bytes 3145732
  19.5 35.6 %copy-start.1 = (bf16[2048,256]{1,0:T(8,128)(2,1)S(1)}, bf16[2048,256]{1,0:T(8,128)(2,1)}, u32[]{:S(2)}) copy-start(bf16[2048,256]{1,0:T(8,128)(2,1)} %constant.25.clone.bv_high) | copy-start | bytes 3145732
